TPU v7x, 128 devices: a whole 4x4x4 slice. The times are simulated.
128 devices in a mesh: guide: 2 (over core), tensor: 16 (over y, x), batch: 4 (over z).
Axes of the slice: x: 4, y: 4, z: 4, core: 2. Of those that a mesh axis runs over, the one named last changes fastest.
Arguments:
- stream: bfloat16 [2, 512, 2048], P('guide', ('batch', 'tensor')), may hold values from -6 to 6
- attn_gain: float32 [2048], replicated, may hold values from 0.25 to 1.75
- w_qkv: bfloat16 [2048, 3072], P(None, 'tensor'), may hold values from -0.125 to 0.125
- cache_keys: bfloat16 [2, 512, 1024, 512], P('guide', ('batch', 'tensor')), may hold values from -600 to 600
- cache_values: bfloat16 [2, 512, 1024, 512], P('guide', ('batch', 'tensor')), may hold values from -6 to 6
- cache_len: int32 [2, 512], P('guide', ('batch', 'tensor')), may hold values from 1 to 1024, as said below
- w_out: bfloat16 [2048, 2048], P('tensor'), may hold values from -0.125 to 0.125
- mlp_gain: float32 [2048], replicated, may hold values from 0.25 to 1.75
- w_gate: bfloat16 [2048, 8192], P(None, 'tensor'), may hold values from -0.125 to 0.125
- w_up: bfloat16 [2048, 8192], P(None, 'tensor'), may hold values from -0.125 to 0.125
- w_down: bfloat16 [8192, 2048], P('tensor'), may hold values from -0.0625 to 0.0625
- final_gain: float32 [2048], replicated, may hold values from 0.25 to 1.75
- lm_head: bfloat16 [65536, 2048], P(('guide', 'tensor')), may hold values from -128 to 128
- next_gain: float32 [2048], replicated, may hold values from 0.25 to 1.75
- w_next: bfloat16 [2048, 3072], P(None, 'tensor'), may hold values from -0.125 to 0.125
- tenant_counts: int32 [4], replicated, may hold values from 1 to 256, 512 in all
- guide_level: int32 [4], replicated, may hold values from 4 to 16
Outputs:
- logprobs: float32 [512, 65536], P('batch', ('guide', 'tensor'))
- layer_out: bfloat16 [2, 512, 2048], P('guide', ('batch', 'tensor'))
- next_qkv: bfloat16 [2, 512, 3072], P('guide', 'batch', 'tensor')
Inputs may be any that keep to these rules, and one draw needn't show every extreme that they name: `cache_len`: in each branch some request has 1024 cached tokens.
All inputs are finite; a program needn't handle non-finite values.
Results may differ from a plain program's by a relative error of at most 0.024.
Values may be sent and summed in bfloat16 or wider, within the bound.
A program may use at most 128 MiB of HBM per device.

v0:
```python
import math

import jax
import jax.numpy as jnp
from jax import lax
from jax.sharding import PartitionSpec as P

D = 2048
HEADS = 32
KV_HEADS = 8
HEAD_DIM = 64
TENANTS = 4


EPSILON = 1e-05
ROPE_BASE = 500000.0
MASKED = -1e30


def from_partner(block, axis, bit):
    count = lax.axis_size(axis)
    route = []
    for low in range(count):
        high = low | 1 << bit
        if high != low and high < count:
            route += [(low, high), (high, low)]
    return lax.ppermute(block, axis, route)


def rms_norm(values, gain):
    widened = values.astype(jnp.float32)
    factor = lax.rsqrt(jnp.mean(widened * widened, axis=-1, keepdims=True) + EPSILON)
    return (widened * factor * gain).astype(jnp.bfloat16)


def scaled_freq(head_size):
    half_dim = head_size // 2
    steps_up = jnp.arange(half_dim, dtype=jnp.float32)
    base_freq = jnp.exp(steps_up * (-2.0 * math.log(ROPE_BASE) / head_size))
    wavelen = 2.0 * math.pi / base_freq
    smooth = (8192.0 / wavelen - 1.0) / 3.0
    middle = (1.0 - smooth) * base_freq / 32.0 + smooth * base_freq
    return jnp.where(
        wavelen < 2048.0, base_freq, jnp.where(wavelen > 8192.0, base_freq / 32.0, middle)
    )


def rotate(values, position):
    half_dim = values.shape[-1] // 2
    freq = scaled_freq(values.shape[-1])
    angle = position * freq
    cosine = jnp.cos(angle)
    sine = jnp.sin(angle)
    first = values[..., :half_dim].astype(jnp.float32)
    second = values[..., half_dim:].astype(jnp.float32)
    joined = jnp.concatenate(
        [first * cosine - second * sine, second * cosine + first * sine], axis=-1
    )
    return joined.astype(jnp.bfloat16)


def swiglu(normed, w_gate, w_up):
    gate = jnp.dot(normed, w_gate, preferred_element_type=jnp.float32)
    upward = jnp.dot(normed, w_up, preferred_element_type=jnp.float32)
    return (jax.nn.silu(gate) * upward).astype(jnp.bfloat16)


def attend(request_side, keys, values, lengths):
    count = request_side.shape[0]
    kv_width = KV_HEADS * HEAD_DIM
    per_group = HEADS // KV_HEADS
    scale = HEAD_DIM ** (-0.5)
    slot_count = keys.shape[1]
    position = lengths.astype(jnp.float32)[:, None, None]
    queries = rotate(request_side[:, :D].reshape(count, HEADS, HEAD_DIM), position)
    queries = queries.reshape(count, KV_HEADS, per_group, HEAD_DIM)
    new_keys = rotate(
        request_side[:, D : D + kv_width].reshape(count, KV_HEADS, HEAD_DIM), position
    )
    new_values = request_side[:, D + kv_width :].reshape(count, KV_HEADS, HEAD_DIM)
    keys_split = keys.reshape(count, slot_count, KV_HEADS, HEAD_DIM)
    values_split = values.reshape(count, slot_count, KV_HEADS, HEAD_DIM)
    fresh = (
        jnp.einsum("rkgd,rkd->rkg", queries, new_keys, preferred_element_type=jnp.float32) * scale
    )
    slots = jnp.arange(slot_count, dtype=jnp.int32)
    live_mask = (slots[None, :] < lengths[:, None])[:, None, None, :]
    scores = (
        jnp.einsum("rkgd,rlkd->rkgl", queries, keys_split, preferred_element_type=jnp.float32)
        * scale
    )
    scores = jnp.where(live_mask, scores, MASKED)
    peak = jnp.maximum(jnp.max(scores, axis=-1), fresh)
    expd = jnp.where(live_mask, jnp.exp(scores - peak[..., None]), 0.0)
    total = jnp.sum(expd, axis=-1)
    weighted = jnp.einsum(
        "rkgl,rlkd->rkgd",
        expd.astype(jnp.bfloat16),
        values_split,
        preferred_element_type=jnp.float32,
    )
    fresh_exp = jnp.exp(fresh - peak)
    total = total + fresh_exp
    fresh_prob = fresh_exp.astype(jnp.bfloat16).astype(jnp.float32)
    weighted = weighted + fresh_prob[..., None] * new_values.astype(jnp.float32)[:, :, None, :]
    return (weighted / total[..., None]).reshape(count, D).astype(jnp.bfloat16)


def local(
    stream,
    attn_gain,
    w_qkv,
    cache_keys,
    cache_values,
    cache_len,
    w_out,
    mlp_gain,
    w_gate,
    w_up,
    w_down,
    final_gain,
    lm_head,
    next_gain,
    w_next,
    tenant_counts,
    guide_level,
):
    own_rows = stream[0]
    projected = jnp.dot(
        lax.all_gather(rms_norm(own_rows, attn_gain), "tensor", axis=0, tiled=True),
        w_qkv,
        preferred_element_type=jnp.float32,
    ).astype(jnp.bfloat16)
    request_side = lax.all_to_all(projected, "tensor", split_axis=0, concat_axis=1, tiled=True)
    mixed = attend(request_side, cache_keys[0], cache_values[0], cache_len[0])
    head_side = lax.all_to_all(mixed, "tensor", split_axis=1, concat_axis=0, tiled=True)
    selected = head_side
    attn_share = lax.psum_scatter(
        jnp.dot(selected, w_out, preferred_element_type=jnp.float32).astype(jnp.bfloat16),
        "tensor",
        scatter_dimension=0,
        tiled=True,
    ).astype(jnp.float32)
    after_attn = (own_rows.astype(jnp.float32) + attn_share).astype(jnp.bfloat16)
    hidden = swiglu(
        lax.all_gather(rms_norm(after_attn, mlp_gain), "tensor", axis=0, tiled=True), w_gate, w_up
    )
    selected = hidden
    mlp_share = lax.psum_scatter(
        jnp.dot(selected, w_down, preferred_element_type=jnp.float32).astype(jnp.bfloat16),
        "tensor",
        scatter_dimension=0,
        tiled=True,
    ).astype(jnp.float32)
    layer_rows = (after_attn.astype(jnp.float32) + mlp_share).astype(jnp.bfloat16)
    all_out = lax.all_gather(layer_rows, "tensor", axis=0, tiled=True)
    next_rows = jnp.dot(
        rms_norm(all_out, next_gain), w_next, preferred_element_type=jnp.float32
    ).astype(jnp.bfloat16)
    final = rms_norm(all_out, final_gain)
    partner = from_partner(final, "guide", 0)
    is_cond = lax.axis_index("guide") == 0
    cond_rows = jnp.where(is_cond, final, partner)
    uncond_rows = jnp.where(is_cond, partner, final)
    batch_rows = final.shape[0]
    logits = lax.dot_general(
        jnp.concatenate([cond_rows, uncond_rows], axis=0),
        lm_head,
        (((1,), (1,)), ((), ())),
        preferred_element_type=jnp.float32,
    )
    cond_logits = logits[:batch_rows]
    uncond_logits = logits[batch_rows:]
    bounds = jnp.cumsum(tenant_counts)[:-1]
    request_ids = lax.axis_index("batch") * batch_rows + jnp.arange(batch_rows, dtype=jnp.int32)
    tenant = jnp.sum((request_ids[:, None] >= bounds[None, :]).astype(jnp.int32), axis=1)
    chosen = (tenant[:, None] == jnp.arange(TENANTS, dtype=jnp.int32)[None, :]).astype(jnp.float32)
    weight = jnp.sum(chosen * guide_level.astype(jnp.float32)[None, :], axis=1) * 0.25
    guided = uncond_logits + weight[:, None] * (cond_logits - uncond_logits)
    peak = lax.pmax(jnp.max(guided, axis=1), ("guide", "tensor"))
    mass = lax.psum(jnp.sum(jnp.exp(guided - peak[:, None]), axis=1), ("guide", "tensor"))
    logprobs = guided - peak[:, None] - jnp.log(mass)[:, None]
    return (logprobs, layer_rows[None], next_rows[None])


def solution(mesh):
    in_specs = (
        P("guide", ("batch", "tensor"), None),
        P(),
        P(None, "tensor"),
        P("guide", ("batch", "tensor"), None, None),
        P("guide", ("batch", "tensor"), None, None),
        P("guide", ("batch", "tensor")),
        P("tensor", None),
        P(),
        P(None, "tensor"),
        P(None, "tensor"),
        P("tensor", None),
        P(),
        P(("guide", "tensor"), None),
        P(),
        P(None, "tensor"),
        P(),
        P(),
    )
    out_specs = (
        P("batch", ("guide", "tensor")),
        P("guide", ("batch", "tensor"), None),
        P("guide", "batch", "tensor"),
    )
    return jax.shard_map(local, mesh=mesh, in_specs=in_specs, out_specs=out_specs, check_vma=False)
```

profile of v0, /device:TPU:1, one launch (start us, length us, event | category | flops | bytes accessed | tf_op | source)
XLA Modules:
  0.0 462.2 jit_solution(6862168536438569131)
XLA Ops:
  7.2 0.0 copy-start
  7.2 0.0 copy-start.5
  7.2 1.0 fusion.39
  8.2 0.8 fusion.41
  9.1 20.0 %all_gather.9 = bf16[128,2048]{1,0:T(8,128)(2,1)S(1)} all-gather(bf16[8,2048]{1,0:T(8,128)(2,1)S(1)} %fusion.41), channel_id=1, replica_groups=mesh['guide'=2,'tensor'=16,'batch'=4] {'tensor'}, dimensions={0}, use_global_device_ids=true | all-gather | bytes 557056 | tf_op jit(solution)/shard_map/all_gather | solution.py:130
  29.0 1.5 convolution_convert_fusion.3
  30.5 0.7 copy.32
  31.3 4.7 %all-to-all-start = ((bf16[16,8,192]{2,1,0:T(8,128)(2,1)}), bf16[16,8,192]{2,1,0:T(8,128)(2,1)S(1)}, u32[]{:S(2)}, u32[]{:S(2)}) async-start(bf16[16,8,192]{2,1,0:T(8,128)(2,1)} %bitcast.3), calls=%async_computation | async-start | bytes 131072 | tf_op jit(solution)/shard_map/all_to_all | solution.py:134
  36.0 0.0 all-reduce.5.cloned.1.call-start
  36.0 0.0 copy-done.5
  36.1 0.1 multiply_cosine_fusion
  36.2 0.1 iota_compare_fusion
  36.3 11.4 %copy.34 = bf16[1,8,1024,512]{2,3,1,0:T(8,128)(2,1)} copy(bf16[1,8,1024,512]{3,2,1,0:T(8,128)(2,1)} %param.20) | data formatting | bytes 16777216 | tf_op args[3]
  47.7 11.5 %copy.35 = bf16[1,8,1024,512]{2,3,1,0:T(8,128)(2,1)} copy(bf16[1,8,1024,512]{3,2,1,0:T(8,128)(2,1)} %param.21) | data formatting | bytes 16777216 | tf_op args[4]
  59.1 0.0 all-to-all-done
  59.2 0.1 all_to_all.29
  59.3 0.1 reshape.189
  59.4 0.1 reshape.188
  59.5 0.1 fusion.44
  59.6 0.1 fusion.31
  59.7 0.1 maximum_bitcast_fusion
  59.8 0.3 fusion.48
  60.1 4.8 %fusion.57 = (f32[8,8,4]{2,1,0:T(8,128)S(1)}, f32[8,8,4,1024]{3,2,1,0:T(4,128)S(1)}) fusion(bf16[8,1024,8,64]{1,3,2,0:T(8,128)(2,1)} %bitcast.42, bf16[8,8,4,32]{3,2,1,0:T(4,128)(2,1)S(1)} %bitcast.47, bf16[8,8,4,32]{3,2,1,0:T(4,128)(2,1)S(1)} %bitcast.45, pred[8,1024]{1,0:T(8,128)(4,1)S(1)} %iota_compare_fusion), kind=kOutput, calls=%fused_computation.103 | convolution fusion | flops 34406144 | bytes 9479168 | tf_op jit(solution)/shard_map/rkgd,rlkd->rkgl/dot_general | solution.py:89
  64.8 0.6 fusion.16
  65.5 0.1 reshape.192
  65.6 5.8 %fusion.5 = bf16[8,8,4,64]{3,2,1,0:T(4,128)(2,1)S(1)} fusion(bf16[8,1024,8,64]{1,3,2,0:T(8,128)(2,1)} %bitcast.43, f32[8,8,4,1024]{3,2,1,0:T(4,128)S(1)} %get-tuple-element.20, f32[8,8,4]{2,1,0:T(8,128)S(1)} %multiply_maximum_fusion, pred[8,1024]{1,0:T(8,128)(4,1)S(1)} %iota_compare_fusion, f32[8,8,4]{2,1,0:T(8,128)S(1)} %get-tuple-element.12, ...), kind=kOutput, calls=%fused_computation.12 | convolution fusion | flops 34406400 | bytes 9497600 | tf_op jit(solution)/shard_map/rkgl,rlkd->rkgd/dot_general | solution.py:96
  71.3 0.1 convert_element_type.124
  71.5 12.9 %all_to_all.35 = bf16[8,16,128]{2,0,1:T(8,128)(2,1)S(1)} all-to-all(bf16[8,16,128]{2,0,1:T(8,128)(2,1)S(1)} %copy.36), channel_id=1, replica_groups=mesh['guide'=2,'tensor'=16,'batch'=4] {'tensor'}, dimensions={1} | all-to-all | bytes 65536 | tf_op jit(solution)/shard_map/all_to_all | solution.py:136
  84.4 2.1 convolution_convert_fusion.1
  86.5 0.0 all-reduce.5.cloned.1.call-update
  86.5 0.0 all-reduce.7.cloned.1.call-start
  86.6 0.0 copy-done.9
  86.6 0.6 dynamic-slice
  87.8 88.3 %all-reduce.5.cloned.1.call-done = bf16[128,2048]{1,0:T(8,128)(2,1)} async-done(((bf16[128,2048]{1,0:T(8,128)(2,1)}), bf16[128,2048]{1,0:T(8,128)(2,1)}) %all-reduce.5.cloned.1.call-update) | async-done | bytes 524304
  176.1 0.0 copy-done.1
  176.1 0.9 fusion.35
  177.0 0.0 copy-done.4
  177.0 0.1 fusion.37
  177.1 17.4 %all_gather.10 = bf16[128,2048]{1,0:T(8,128)(2,1)S(1)} all-gather(bf16[8,2048]{1,0:T(8,128)(2,1)S(1)} %fusion.37), channel_id=1, replica_groups=mesh['guide'=2,'tensor'=16,'batch'=4] {'tensor'}, dimensions={0}, use_global_device_ids=true | all-gather | bytes 557056 | tf_op jit(solution)/shard_map/all_gather | solution.py:146
  194.5 2.0 fusion.58
  196.6 0.0 copy-done
  196.6 0.0 copy-start.7
  196.6 0.0 copy-start.3
  196.6 3.2 convolution_convert_fusion
  199.8 0.0 all-reduce.7.cloned.1.call-update
  199.9 0.2 reduce-window.4
  200.1 0.1 convert_reduce_fusion
  200.2 89.2 %all-reduce.7.cloned.1.call-done = bf16[128,2048]{1,0:T(8,128)(2,1)} async-done(((bf16[128,2048]{1,0:T(8,128)(2,1)}), bf16[128,2048]{1,0:T(8,128)(2,1)}) %all-reduce.7.cloned.1.call-update) | async-done | bytes 524304
  289.3 0.8 fusion.38
  290.1 0.0 copy-start.2
  290.1 17.4 %all_gather.11 = bf16[128,2048]{1,0:T(8,128)(2,1)S(1)} all-gather(bf16[8,2048]{1,0:T(8,128)(2,1)S(1)} %fusion.38), channel_id=1, replica_groups=mesh['guide'=2,'tensor'=16,'batch'=4] {'tensor'}, dimensions={0}, use_global_device_ids=true | all-gather | bytes 557056 | tf_op jit(solution)/shard_map/all_gather | solution.py:156
  307.5 0.2 fusion.9
  307.7 0.2 fusion.7
  307.9 8.1 %collective-permute-start = (bf16[128,2048]{1,0:T(8,128)(2,1)S(1)}, bf16[128,2048]{1,0:T(8,128)(2,1)}, u32[]{:S(2)}, u32[]{:S(2)}) collective-permute-start(bf16[128,2048]{1,0:T(8,128)(2,1)S(1)} %fusion.7), channel_id=1, source_target_pairs={{0,64},{64,0},{1,65},{65,1},{2,66},{66,2},{3,67},{67,3},{4,68},{68... | collective-permute-start | bytes 1572872 | tf_op jit(solution)/shard_map/ppermute | solution.py:27
  316.1 0.1 select_reduce_fusion
  316.1 2.2 fusion.6
  318.4 0.0 collective-permute-done
  318.4 1.4 broadcast_select_fusion.1
  319.8 5.7 %fusion.12 = f32[256,2048]{1,0:T(8,128)S(1)} fusion(bf16[2048,2048]{1,0:T(8,128)(2,1)} %param.29, bf16[128,2048]{1,0:T(8,128)(2,1)S(1)} %get-tuple-element.8, bf16[128,2048]{1,0:T(8,128)(2,1)S(1)} %get-tuple-element.7), kind=kOutput, calls=%fused_computation.22 | convolution fusion | flops 2149580800 | bytes 11534336 | tf_op jit(solution)/shard_map/dot_general | solution.py:166
  325.5 0.4 fusion.54
  326.0 65.0 %pmax.7 = f32[128]{0:T(128)S(1)} all-reduce(f32[128]{0:T(128)S(1)} %get-tuple-element.3), channel_id=1, replica_groups=mesh['guide'=2,'tensor'=16,'batch'=4] {'guide','tensor'}, use_global_device_ids=true, to_apply=%region_11.12 | all-reduce | flops 128 | bytes 1024 | tf_op jit(solution)/shard_map/pmax | solution.py:180
  391.0 0.3 exponential_reduce_fusion
  391.3 62.9 %psum.7 = f32[128]{0:T(128)S(1)} all-reduce(f32[128]{0:T(128)S(1)} %exponential_reduce_fusion), channel_id=1, replica_groups=mesh['guide'=2,'tensor'=16,'batch'=4] {'guide','tensor'}, use_global_device_ids=true, to_apply=%region_13.14 | all-reduce | flops 128 | bytes 1024 | tf_op jit(solution)/shard_map/psum | solution.py:181
  454.2 1.1 subtract_subtract_fusion
  (26 shorter events, 0.1 us)
Async XLA Ops:
  7.2 189.4 %copy-start = (bf16[512,2048]{1,0:T(8,128)(2,1)S(1)}, bf16[512,2048]{1,0:T(8,128)(2,1)}, u32[]{:S(2)}) copy-start(bf16[512,2048]{1,0:T(8,128)(2,1)} %param.27) | copy-start | bytes 6291460
  7.2 28.9 %copy-start.5 = (s32[1,8]{1,0:T(1,128)S(1)}, s32[1,8]{1,0:T(1,128)}, u32[]{:S(2)}) copy-start(s32[1,8]{1,0:T(1,128)} %param.22) | copy-start | bytes 100
  31.3 27.9 %all-to-all-start = ((bf16[16,8,192]{2,1,0:T(8,128)(2,1)}), bf16[16,8,192]{2,1,0:T(8,128)(2,1)S(1)}, u32[]{:S(2)}, u32[]{:S(2)}) async-start(bf16[16,8,192]{2,1,0:T(8,128)(2,1)} %bitcast.3), calls=%async_computation | async-start | bytes 131072 | tf_op jit(solution)/shard_map/all_to_all | solution.py:134
  36.0 140.2 %all-reduce.5.cloned.1.call-start = ((), (), s32[]{:S(2)}) async-start(), calls=%async_computation.2 | async-start | bytes 1048576
  65.5 21.1 %copy-start.9 = (u32[128]{0:T(128)S(1)}, u32[128]{0:T(128)}, u32[]{:S(2)}) copy-start(u32[128]{0:T(128)} %constant.67) | copy-start | bytes 1540
  65.5 110.6 %copy-start.1 = (bf16[1,8,2048]{2,1,0:T(8,128)(2,1)S(1)}, bf16[1,8,2048]{2,1,0:T(8,128)(2,1)}, u32[]{:S(2)}) copy-start(bf16[1,8,2048]{2,1,0:T(8,128)(2,1)} %param.17) | copy-start | bytes 98308
  65.6 111.5 %copy-start.4 = (f32[2048]{0:T(1024)S(1)}, f32[2048]{0:T(1024)}, u32[]{:S(2)}) copy-start(f32[2048]{0:T(1024)} %param.24) | copy-start | bytes 24580
  86.5 202.8 %all-reduce.7.cloned.1.call-start = ((), (), s32[]{:S(2)}) async-start(), calls=%async_computation.3 | async-start | bytes 1048576
  196.6 3.3 copy-start.7
  196.6 111.1 %copy-start.3 = (f32[2048]{0:T(1024)S(1)}, f32[2048]{0:T(1024)}, u32[]{:S(2)}) copy-start(f32[2048]{0:T(1024)} %param.28) | copy-start | bytes 24580
  199.8 116.2 %copy-start.8 = (s32[4]{0:T(128)S(1)}, s32[4]{0:T(128)}, u32[]{:S(2)}) copy-start(s32[4]{0:T(128)} %param.33) | copy-start | bytes 52
  199.8 116.3 %copy-start.6 = (f32[2048]{0:T(1024)S(1)}, f32[2048]{0:T(1024)}, u32[]{:S(2)}) copy-start(f32[2048]{0:T(1024)} %param.30) | copy-start | bytes 24580
  290.1 29.7 %copy-start.2 = (bf16[8,2048]{1,0:T(8,128)(2,1)}, bf16[8,2048]{1,0:T(8,128)(2,1)S(1)}, u32[]{:S(2)}) copy-start(bf16[8,2048]{1,0:T(8,128)(2,1)S(1)} %fusion.38) | copy-start | bytes 98308
  307.9 10.4 %collective-permute-start = (bf16[128,2048]{1,0:T(8,128)(2,1)S(1)}, bf16[128,2048]{1,0:T(8,128)(2,1)}, u32[]{:S(2)}, u32[]{:S(2)}) collective-permute-start(bf16[128,2048]{1,0:T(8,128)(2,1)S(1)} %fusion.7), channel_id=1, source_target_pairs={{0,64},{64,0},{1,65},{65,1},{2,66},{66,2},{3,67},{67,3},{4,68},{68... | collective-permute-start | bytes 1572872 | tf_op jit(solution)/shard_map/ppermute | solution.py:27
Sparse Core Ops, SparseCore 0:
  86.7 89.4 all-reduce.4
  200.0 89.2 all-reduce.6
where the time goes:
time: 464 us; the launch traced here: 462 us
  blocking collectives  196 us (42%)
  waiting for transfers between devices  178 us (38%)
  matrix products  27.7 us (6%)
  local copies, waits for them, and re-layouts  24.8 us (5%)
  between operations  14.9 us (3%)
  starting transfers between devices  12.9 us (3%)
  other arithmetic  8.77 us (2%)
    unnamed x4, waiting for transfers between devices  177 us
    pmax x1, blocking collectives, local(): peak = lax.pmax(jnp.max(guided, axis=1), ('guide', 'tensor'))  65 us
    psum x1, blocking collectives, local(): lax.psum(jnp.sum(jnp.exp(guided - peak[:, None]), axis=1), ('guide', 'ten...  62.9 us
    unnamed x23, local copies, waits for them, and re-layouts  23.5 us
    all_gather x1, blocking collectives, local(): lax.all_gather(rms_norm(own_rows, attn_gain), 'tensor', axis=0, tiled=True)  20 us
    all_gather x1, blocking collectives, local(): all_out = lax.all_gather(layer_rows, 'tensor', axis=0, tiled=True)  17.4 us
    all_gather x1, blocking collectives, local(): lax.all_gather(rms_norm(after_attn, mlp_gain), 'tensor', axis=0, tiled=True)  17.4 us
    all_to_all x1, blocking collectives, local(): lax.all_to_all(mixed, 'tensor', split_axis=1, concat_axis=0, tiled=True)  12.9 us
  transfers between devices with their start and end apart: 4, of which 2 were waited for; matrix products, arithmetic and copies ran while one was open for 6% of the time, Pallas kernels for 0%

commit v1 on v0

v1 whole, which is shorter than its diff:
```python
import functools
import math

import jax
import jax.numpy as jnp
from jax import lax
from jax.experimental import pallas as pl
from jax.experimental.pallas import tpu as pltpu
from jax.sharding import PartitionSpec as P

D = 2048
HALF = D // 2
HEADS = 32
KV_HEADS = 8
GROUPS = HEADS // KV_HEADS
HEAD_DIM = 64
KV_WIDTH = KV_HEADS * HEAD_DIM
TENANTS = 4
SLOTS = 1024
FF_LOCAL = 512
QKV_LOCAL = 192
VOCAB_LOCAL = 2048
ROWS = 128
OWN = 8
SIDE = 4
TENSOR = 16
GUIDE = 2
VOCAB_STEP = 256

EPSILON = 1e-05
ROPE_BASE = 500000.0
MASKED = -1e30
MESH = pl.DeviceIdType.MESH
F32 = jnp.float32
BF16 = jnp.bfloat16
LOW = pl.ds(0, HALF)
HIGH = pl.ds(HALF, HALF)
NT = (((1,), (1,)), ((), ()))


def norm_factor(wide):
    return lax.rsqrt(jnp.mean(wide * wide, axis=-1, keepdims=True) + EPSILON)


def rms_norm(wide, gain):
    return wide * norm_factor(wide) * gain


def lane_freq(shape):
    lane = lax.broadcasted_iota(jnp.int32, shape, 1)
    steps_up = (lane % (HEAD_DIM // 2)).astype(F32)
    base_freq = jnp.exp(steps_up * (-2.0 * math.log(ROPE_BASE) / HEAD_DIM))
    wavelen = 2.0 * math.pi / base_freq
    smooth = (8192.0 / wavelen - 1.0) / 3.0
    middle = (1.0 - smooth) * base_freq / 32.0 + smooth * base_freq
    return jnp.where(
        wavelen < 2048.0, base_freq, jnp.where(wavelen > 8192.0, base_freq / 32.0, middle)
    )


def rotate(wide, cosine, sine, first):
    width = wide.shape[-1]
    ahead = pltpu.roll(wide, width - HEAD_DIM // 2, 1)
    behind = pltpu.roll(wide, HEAD_DIM // 2, 1)
    return wide * cosine + jnp.where(first, -ahead, behind) * sine


def spread(block):
    return block.astype(F32).reshape(-1, block.shape[-1]).astype(BF16)


def drain(ref, sem):
    pltpu.make_async_copy(ref, ref, sem).wait()


def send(src, dst, send_sem, recv_sem, device):
    pltpu.make_async_remote_copy(
        src_ref=src,
        dst_ref=dst,
        send_sem=send_sem,
        recv_sem=recv_sem,
        device_id=device,
        device_id_type=MESH,
    ).start()


def gather_first(buf, y, x, sends, recvs):
    for step in (2, 1, 3):
        there = lax.rem(x + step, SIDE)
        own = buf.at[y, x, :, LOW]
        send(own, own, sends.at[0], recvs.at[0], {"tensor": y * SIDE + there})
        there = lax.rem(y + step, SIDE)
        own = buf.at[y, x, :, HIGH]
        send(own, own, sends.at[1], recvs.at[1], {"tensor": there * SIDE + x})


def gather_second(buf, y, x, sends, recvs):
    part = buf.at[0, pl.ds(0, SIDE - 1), :, LOW]
    drain(part, recvs.at[0])
    for step in (2, 1, 3):
        there = lax.rem(y + step, SIDE)
        row = buf.at[y, :, :, LOW]
        send(row, row, sends.at[2], recvs.at[2], {"tensor": there * SIDE + x})
    drain(part, recvs.at[1])
    for step in (2, 1, 3):
        there = lax.rem(x + step, SIDE)
        column = buf.at[:, x, :, HIGH]
        send(column, column, sends.at[3], recvs.at[3], {"tensor": y * SIDE + there})


def gather_low(buf, recvs):
    drain(buf.at[pl.ds(0, SIDE - 1), :, :, LOW], recvs.at[2])


def gather_high(buf, recvs):
    drain(buf.at[pl.ds(0, SIDE - 1), :, :, LOW], recvs.at[3])


def gather_sent(buf, sends):
    part = buf.at[0, pl.ds(0, SIDE - 1), :, LOW]
    drain(part, sends.at[0])
    drain(part, sends.at[1])
    whole = buf.at[pl.ds(0, SIDE - 1), :, :, LOW]
    drain(whole, sends.at[2])
    drain(whole, sends.at[3])


def all_gather(buf, y, x, sends, recvs):
    gather_first(buf, y, x, sends, recvs)
    gather_second(buf, y, x, sends, recvs)
    gather_low(buf, recvs)
    gather_high(buf, recvs)


def reduce_scatter(partial, first_low, first_high, mid_low, mid_high, last_low, last_high, y, x, sends, recvs):
    for step in (2, 1, 3):
        there = lax.rem(x + step, SIDE)
        send(
            partial.at[:, there, :, LOW], first_low.at[step - 1], sends.at[0], recvs.at[0],
            {"tensor": y * SIDE + there},
        )
        there = lax.rem(y + step, SIDE)
        send(
            partial.at[there, :, :, HIGH], first_high.at[step - 1], sends.at[1], recvs.at[1],
            {"tensor": there * SIDE + x},
        )
    drain(first_low, recvs.at[0])
    for at in range(SIDE):
        part = partial[at, x, :, LOW].astype(F32)
        for k in range(SIDE - 1):
            part = part + first_low[k, at].astype(F32)
        mid_low[at] = part.astype(BF16)
    for step in (2, 1, 3):
        there = lax.rem(y + step, SIDE)
        send(
            mid_low.at[there], last_low.at[step - 1], sends.at[2], recvs.at[2],
            {"tensor": there * SIDE + x},
        )
    drain(first_high, recvs.at[1])
    for at in range(SIDE):
        part = partial[y, at, :, HIGH].astype(F32)
        for k in range(SIDE - 1):
            part = part + first_high[k, at].astype(F32)
        mid_high[at] = part.astype(BF16)
    for step in (2, 1, 3):
        there = lax.rem(x + step, SIDE)
        send(
            mid_high.at[there], last_high.at[step - 1], sends.at[3], recvs.at[3],
            {"tensor": y * SIDE + there},
        )
    drain(last_low, recvs.at[2])
    low = mid_low[y].astype(F32)
    for k in range(SIDE - 1):
        low = low + last_low[k].astype(F32)
    drain(last_high, recvs.at[3])
    high = mid_high[x].astype(F32)
    for k in range(SIDE - 1):
        high = high + last_high[k].astype(F32)
    return jnp.concatenate([low, high], axis=1)


def scatter_sent(first_low, first_high, last_low, last_high, sends):
    drain(first_low, sends.at[0])
    drain(first_high, sends.at[1])
    drain(last_low, sends.at[2])
    drain(last_high, sends.at[3])


def exchange(src, dst, me, send_sem, recv_sem):
    dst[me] = src[me]
    for step in range(1, TENSOR):
        there = lax.rem(me + step, TENSOR)
        send(src.at[there], dst.at[me], send_sem, recv_sem, {"tensor": there})


def kernel(
    stream, attn_gain, w_qkv, keys, values, lengths, w_out, mlp_gain, w_gate, w_up, w_down,
    final_gain, lm_head, next_gain, w_next, counts, levels,
    logprobs, layer_out, next_qkv,
    stream_v, gains_v, w_qkv_v, keys_v, values_v, w_out_v, w_gate_v, w_up_v, w_down_v, lm_head_v, w_next_v,
    gather_a, gather_b, gather_c, other_c, proj, request_side, queries, mixed, head_out, head_in,
    partial, first_low, first_high, mid_low, mid_high, last_low, last_high,
    final_rows, next_rows, stats_own, stats_all,
    load_sems, ag_send, ag_recv, rs_send, rs_recv, a2a_send, a2a_recv, pair_send, pair_recv,
):
    guide = lax.axis_index("guide")
    me = lax.axis_index("tensor")
    batch = lax.axis_index("batch")
    y = me // SIDE
    x = lax.rem(me, SIDE)
    other = 1 - guide

    loads = [
        pltpu.make_async_copy(stream.at[0], stream_v, load_sems.at[0]),
        pltpu.make_async_copy(attn_gain, gains_v.at[0], load_sems.at[1]),
        pltpu.make_async_copy(w_qkv, w_qkv_v, load_sems.at[2]),
        pltpu.make_async_copy(keys.at[0], keys_v, load_sems.at[3]),
        pltpu.make_async_copy(values.at[0], values_v, load_sems.at[4]),
        pltpu.make_async_copy(w_out, w_out_v, load_sems.at[5]),
        pltpu.make_async_copy(mlp_gain, gains_v.at[1], load_sems.at[6]),
        pltpu.make_async_copy(w_gate, w_gate_v, load_sems.at[7]),
        pltpu.make_async_copy(w_up, w_up_v, load_sems.at[8]),
        pltpu.make_async_copy(w_down, w_down_v, load_sems.at[9]),
        pltpu.make_async_copy(next_gain, gains_v.at[2], load_sems.at[10]),
        pltpu.make_async_copy(final_gain, gains_v.at[3], load_sems.at[11]),
        pltpu.make_async_copy(w_next, w_next_v, load_sems.at[12]),
        pltpu.make_async_copy(lm_head, lm_head_v, load_sems.at[13]),
    ]
    for load in loads:
        load.start()

    barrier = pltpu.get_barrier_semaphore()
    for step in range(1, TENSOR):
        there = lax.rem(me + step, TENSOR)
        pl.semaphore_signal(barrier, inc=1, device_id={"tensor": there}, device_id_type=MESH)
    for there in range(TENSOR):
        pl.semaphore_signal(
            barrier, inc=1, device_id={"guide": other, "tensor": there}, device_id_type=MESH
        )

    loads[0].wait()
    loads[1].wait()
    own_rows = stream_v[...].astype(F32)
    gather_a[y, x] = rms_norm(own_rows, gains_v[0]).astype(BF16)
    pl.semaphore_wait(barrier, 2 * TENSOR - 1)

    gather_first(gather_a, y, x, ag_send.at[0], ag_recv.at[0])
    row = lax.broadcasted_iota(jnp.int32, (OWN, 2 * HEAD_DIM), 0)
    position = jnp.zeros((OWN, 2 * HEAD_DIM), F32)
    for r in range(OWN):
        position = jnp.where(row == r, lengths[0, r].astype(F32), position)
    angle = position * lane_freq((OWN, 2 * HEAD_DIM))
    cosine = jnp.concatenate([jnp.cos(angle)] * (KV_WIDTH // (2 * HEAD_DIM)), axis=1)
    sine = jnp.concatenate([jnp.sin(angle)] * (KV_WIDTH // (2 * HEAD_DIM)), axis=1)
    gather_second(gather_a, y, x, ag_send.at[0], ag_recv.at[0])
    loads[2].wait()
    gather_low(gather_a, ag_recv.at[0])
    gather_high(gather_a, ag_recv.at[0])

    rows = spread(gather_a[...])
    projected = jnp.dot(rows, w_qkv_v[...], preferred_element_type=F32)
    proj[:, :, 0:QKV_LOCAL] = projected.reshape(TENSOR, OWN, QKV_LOCAL).astype(BF16)
    exchange(proj, request_side, me, a2a_send.at[0], a2a_recv.at[0])
    drain(request_side.at[pl.ds(0, TENSOR - 1)], a2a_recv.at[0])

    def piece(column):
        at, j = divmod(column, 3)
        return request_side[at, :, j * HEAD_DIM : (j + 1) * HEAD_DIM].astype(F32)

    lane = lax.broadcasted_iota(jnp.int32, (OWN, KV_WIDTH), 1)
    first = lax.rem(lane, HEAD_DIM) < HEAD_DIM // 2
    for g in range(GROUPS):
        wide = jnp.concatenate([piece(GROUPS * k + g) for k in range(KV_HEADS)], axis=1)
        queries[g] = rotate(wide, cosine, sine, first).astype(BF16).astype(F32) * (HEAD_DIM**-0.5)
    wide = jnp.concatenate([piece(HEADS + k) for k in range(KV_HEADS)], axis=1)
    queries[GROUPS] = rotate(wide, cosine, sine, first).astype(BF16).astype(F32)
    queries[GROUPS + 1] = jnp.concatenate(
        [piece(HEADS + KV_HEADS + k) for k in range(KV_HEADS)], axis=1
    )

    loads[3].wait()
    loads[4].wait()
    own_head = lane // HEAD_DIM == lax.broadcasted_iota(jnp.int32, (OWN, KV_WIDTH), 0)
    slot = lax.broadcasted_iota(jnp.int32, (HEADS, SLOTS), 1)

    def attend(r, carry):
        rowed = [
            jnp.where(own_head, jnp.broadcast_to(queries[g, pl.ds(r, 1), :], (KV_HEADS, KV_WIDTH)), 0.0)
            for g in range(GROUPS)
        ]
        spread_q = jnp.concatenate(rowed, axis=0)
        new_key = queries[GROUPS, pl.ds(r, 1), :]
        new_value = queries[GROUPS + 1, pl.ds(r, 1), :]
        scores = lax.dot_general(spread_q.astype(BF16), keys_v[r], NT, preferred_element_type=F32)
        fresh = jnp.sum(spread_q * new_key, axis=1, keepdims=True)
        scores = jnp.where(slot < lengths[0, r], scores, MASKED)
        peak = jnp.maximum(jnp.max(scores, axis=1, keepdims=True), fresh)
        expd = jnp.exp(scores - peak)
        fresh_exp = jnp.exp(fresh - peak)
        total = jnp.sum(expd, axis=1, keepdims=True) + fresh_exp
        weighted = jnp.dot(expd.astype(BF16), values_v[r], preferred_element_type=F32)
        weighted = weighted + fresh_exp.astype(BF16).astype(F32) * new_value
        weighted = weighted / total
        for g in range(GROUPS):
            kept = jnp.where(own_head, weighted[g * KV_HEADS : (g + 1) * KV_HEADS], 0.0)
            mixed[g, pl.ds(r, 1), :] = jnp.sum(kept, axis=0, keepdims=True)
        return carry

    lax.fori_loop(0, OWN, attend, 0, unroll=True)

    for at in range(TENSOR):
        k, g = at // 2, (at % 2) * 2
        here = slice(k * HEAD_DIM, (k + 1) * HEAD_DIM)
        head_out[at] = jnp.concatenate([mixed[g, :, here], mixed[g + 1, :, here]], axis=1).astype(BF16)
    exchange(head_out, head_in, me, a2a_send.at[1], a2a_recv.at[1])
    loads[5].wait()
    drain(head_in.at[pl.ds(0, TENSOR - 1)], a2a_recv.at[1])

    terms = jnp.dot(spread(head_in[...]), w_out_v[...], preferred_element_type=F32)
    partial[0] = terms.reshape(SIDE, SIDE, OWN, D).astype(BF16)
    attn_share = reduce_scatter(
        partial.at[0], first_low.at[0], first_high.at[0], mid_low.at[0], mid_high.at[0],
        last_low.at[0], last_high.at[0], y, x, rs_send.at[0], rs_recv.at[0],
    )
    after_attn = (own_rows + attn_share).astype(BF16).astype(F32)
    loads[6].wait()
    gather_b[y, x] = rms_norm(after_attn, gains_v[1]).astype(BF16)
    gather_first(gather_b, y, x, ag_send.at[1], ag_recv.at[1])
    gather_second(gather_b, y, x, ag_send.at[1], ag_recv.at[1])
    for load in loads[7:10]:
        load.wait()
    gather_low(gather_b, ag_recv.at[1])
    gather_high(gather_b, ag_recv.at[1])

    rows = spread(gather_b[...])
    gate = jnp.dot(rows, w_gate_v[...], preferred_element_type=F32)
    upward = jnp.dot(rows, w_up_v[...], preferred_element_type=F32)
    hidden = (gate * jax.nn.sigmoid(gate) * upward).astype(BF16)
    terms = jnp.dot(hidden, w_down_v[...], preferred_element_type=F32)
    partial[1] = terms.reshape(SIDE, SIDE, OWN, D).astype(BF16)
    mlp_share = reduce_scatter(
        partial.at[1], first_low.at[1], first_high.at[1], mid_low.at[1], mid_high.at[1],
        last_low.at[1], last_high.at[1], y, x, rs_send.at[1], rs_recv.at[1],
    )
    layer_rows = (after_attn + mlp_share).astype(BF16)
    layer_out[0] = layer_rows
    gather_c[y, x] = layer_rows
    gather_first(gather_c, y, x, ag_send.at[2], ag_recv.at[2])
    gather_second(gather_c, y, x, ag_send.at[2], ag_recv.at[2])
    for load in loads[10:]:
        load.wait()
    gather_low(gather_c, ag_recv.at[2])
    low = gather_c.at[:, :, :, LOW]
    send(low, other_c.at[:, :, :, LOW], pair_send.at[0], pair_recv.at[0], {"guide": other})
    gather_high(gather_c, ag_recv.at[2])
    high = gather_c.at[:, :, :, HIGH]
    send(high, other_c.at[:, :, :, HIGH], pair_send.at[1], pair_recv.at[1], {"guide": other})

    def norm_own(at, carry):
        wide = gather_c[pl.ds(at, 1)].astype(F32).reshape(SIDE * OWN, D)
        scaled = wide * norm_factor(wide)
        start = pl.multiple_of(at * SIDE * OWN, SIDE * OWN)
        next_rows[pl.ds(start, SIDE * OWN), :] = (scaled * gains_v[2]).astype(BF16)
        final_rows[guide, pl.ds(start, SIDE * OWN), :] = (scaled * gains_v[3]).astype(BF16)
        return carry

    lax.fori_loop(0, SIDE, norm_own, 0)
    next_qkv[0] = jnp.dot(next_rows[...], w_next_v[...], preferred_element_type=F32).astype(BF16)
    drain(low, pair_recv.at[0])
    drain(high, pair_recv.at[1])

    def norm_other(at, carry):
        wide = other_c[pl.ds(at, 1)].astype(F32).reshape(SIDE * OWN, D)
        start = pl.multiple_of(at * SIDE * OWN, SIDE * OWN)
        final_rows[other, pl.ds(start, SIDE * OWN), :] = rms_norm(wide, gains_v[3]).astype(BF16)
        return carry

    lax.fori_loop(0, SIDE, norm_other, 0)

    request = batch * ROWS + lax.broadcasted_iota(jnp.int32, (ROWS, VOCAB_STEP), 0)
    level = jnp.full((ROWS, VOCAB_STEP), levels[0].astype(F32))
    bound = counts[0]
    for t in range(1, TENANTS):
        level = jnp.where(request >= bound, levels[t].astype(F32), level)
        bound = bound + counts[t]
    weight = level * 0.25

    def score(step, top):
        start = pl.multiple_of(step * VOCAB_STEP, VOCAB_STEP)
        logits = lax.dot_general(
            final_rows[...].reshape(GUIDE * ROWS, D), lm_head_v[pl.ds(start, VOCAB_STEP), :], NT,
            preferred_element_type=F32,
        )
        uncond = logits[ROWS:]
        guided = uncond + weight * (logits[:ROWS] - uncond)
        logprobs[:, pl.ds(start, VOCAB_STEP)] = guided
        return jnp.maximum(top, guided)

    top = lax.fori_loop(
        0, VOCAB_LOCAL // VOCAB_STEP, score, jnp.full((ROWS, VOCAB_STEP), -jnp.inf, F32)
    )
    top = jnp.max(top, axis=1, keepdims=True)

    def add_up(step, total):
        start = pl.multiple_of(step * VOCAB_STEP, VOCAB_STEP)
        return total + jnp.exp(logprobs[:, pl.ds(start, VOCAB_STEP)] - top)

    mass = lax.fori_loop(
        0, VOCAB_LOCAL // VOCAB_STEP, add_up, jnp.zeros((ROWS, VOCAB_STEP), F32)
    )
    mass = jnp.sum(mass, axis=1, keepdims=True)
    column = lax.broadcasted_iota(jnp.int32, (ROWS, ROWS), 1)
    packed = jnp.where(column == 0, top, mass)
    place = guide * TENSOR + me
    mine = jnp.transpose(packed)[0:8]
    stats_own[...] = mine
    stats_all[place] = mine
    for step in range(1, TENSOR):
        there = lax.rem(me + step, TENSOR)
        send(stats_own, stats_all.at[place], a2a_send.at[2], a2a_recv.at[2], {"tensor": there})
    for step in range(TENSOR):
        there = lax.rem(me + step, TENSOR)
        send(
            stats_own, stats_all.at[place], a2a_send.at[2], a2a_recv.at[2],
            {"guide": other, "tensor": there},
        )
    drain(stats_all.at[pl.ds(0, GUIDE * TENSOR - 1)], a2a_recv.at[2])
    peaks = stats_all[:, 0, :]
    peak = jnp.max(peaks, axis=0, keepdims=True)
    total = jnp.sum(stats_all[:, 1, :] * jnp.exp(peaks - peak), axis=0, keepdims=True)
    level = jnp.transpose(jnp.broadcast_to(peak + jnp.log(total), (ROWS, ROWS)))
    level = jnp.concatenate([level] * (VOCAB_STEP // ROWS), axis=1)

    def settle(step, carry):
        start = pl.multiple_of(step * VOCAB_STEP, VOCAB_STEP)
        logprobs[:, pl.ds(start, VOCAB_STEP)] = logprobs[:, pl.ds(start, VOCAB_STEP)] - level
        return carry

    lax.fori_loop(0, VOCAB_LOCAL // VOCAB_STEP, settle, 0)

    for k, buf in enumerate((gather_a, gather_b, gather_c)):
        gather_sent(buf, ag_send.at[k])
    for k in range(2):
        scatter_sent(first_low.at[k], first_high.at[k], last_low.at[k], last_high.at[k], rs_send.at[k])
    drain(request_side.at[pl.ds(0, TENSOR - 1)], a2a_send.at[0])
    drain(head_in.at[pl.ds(0, TENSOR - 1)], a2a_send.at[1])
    drain(stats_all.at[pl.ds(0, GUIDE * TENSOR - 1)], a2a_send.at[2])
    drain(low, pair_send.at[0])
    drain(high, pair_send.at[1])


def local(
    stream, attn_gain, w_qkv, cache_keys, cache_values, cache_len, w_out, mlp_gain, w_gate, w_up, w_down,
    final_gain, lm_head, next_gain, w_next, tenant_counts, guide_level,
):
    hbm = pl.BlockSpec(memory_space=pl.ANY)
    smem = pl.BlockSpec(memory_space=pltpu.SMEM)
    vmem = pl.BlockSpec(memory_space=pltpu.VMEM)
    dma = pltpu.SemaphoreType.DMA
    wide = lambda gain: gain.reshape(1, D)
    return pl.pallas_call(
        kernel,
        name="decode_step",
        out_shape=(
            jax.ShapeDtypeStruct((ROWS, VOCAB_LOCAL), F32),
            jax.ShapeDtypeStruct((1, OWN, D), BF16),
            jax.ShapeDtypeStruct((1, ROWS, QKV_LOCAL), BF16),
        ),
        in_specs=[hbm] * 5 + [smem] + [hbm] * 9 + [smem] * 2,
        out_specs=(vmem, vmem, vmem),
        scratch_shapes=[
            pltpu.VMEM((OWN, D), BF16),
            pltpu.VMEM((4, 1, D), F32),
            pltpu.VMEM((D, QKV_LOCAL), BF16),
            pltpu.VMEM((OWN, SLOTS, KV_WIDTH), BF16),
            pltpu.VMEM((OWN, SLOTS, KV_WIDTH), BF16),
            pltpu.VMEM((ROWS, D), BF16),
            pltpu.VMEM((D, FF_LOCAL), BF16),
            pltpu.VMEM((D, FF_LOCAL), BF16),
            pltpu.VMEM((FF_LOCAL, D), BF16),
            pltpu.VMEM((VOCAB_LOCAL, D), BF16),
            pltpu.VMEM((D, QKV_LOCAL), BF16),
            pltpu.VMEM((SIDE, SIDE, OWN, D), BF16),
            pltpu.VMEM((SIDE, SIDE, OWN, D), BF16),
            pltpu.VMEM((SIDE, SIDE, OWN, D), BF16),
            pltpu.VMEM((SIDE, SIDE, OWN, D), BF16),
            pltpu.VMEM((TENSOR, OWN, QKV_LOCAL), BF16),
            pltpu.VMEM((TENSOR, OWN, QKV_LOCAL), BF16),
            pltpu.VMEM((GROUPS + 2, OWN, KV_WIDTH), F32),
            pltpu.VMEM((GROUPS, OWN, KV_WIDTH), F32),
            pltpu.VMEM((TENSOR, OWN, ROWS), BF16),
            pltpu.VMEM((TENSOR, OWN, ROWS), BF16),
            pltpu.VMEM((2, SIDE, SIDE, OWN, D), BF16),
            pltpu.VMEM((2, SIDE - 1, SIDE, OWN, HALF), BF16),
            pltpu.VMEM((2, SIDE - 1, SIDE, OWN, HALF), BF16),
            pltpu.VMEM((2, SIDE, OWN, HALF), BF16),
            pltpu.VMEM((2, SIDE, OWN, HALF), BF16),
            pltpu.VMEM((2, SIDE - 1, OWN, HALF), BF16),
            pltpu.VMEM((2, SIDE - 1, OWN, HALF), BF16),
            pltpu.VMEM((GUIDE, ROWS, D), BF16),
            pltpu.VMEM((ROWS, D), BF16),
            pltpu.VMEM((8, ROWS), F32),
            pltpu.VMEM((GUIDE * TENSOR, 8, ROWS), F32),
            dma((14,)),
            dma((3, 4)),
            dma((3, 4)),
            dma((2, 4)),
            dma((2, 4)),
            dma((3,)),
            dma((3,)),
            dma((2,)),
            dma((2,)),
        ],
        compiler_params=pltpu.CompilerParams(
            collective_id=0, has_side_effects=True, vmem_limit_bytes=60 * 1024 * 1024
        ),
    )(
        stream, wide(attn_gain), w_qkv, cache_keys, cache_values, cache_len, w_out, wide(mlp_gain),
        w_gate, w_up, w_down, wide(final_gain), lm_head, wide(next_gain), w_next, tenant_counts, guide_level,
    )


def solution(mesh):
    in_specs = (
        P("guide", ("batch", "tensor"), None),
        P(),
        P(None, "tensor"),
        P("guide", ("batch", "tensor"), None, None),
        P("guide", ("batch", "tensor"), None, None),
        P("guide", ("batch", "tensor")),
        P("tensor", None),
        P(),
        P(None, "tensor"),
        P(None, "tensor"),
        P("tensor", None),
        P(),
        P(("guide", "tensor"), None),
        P(),
        P(None, "tensor"),
        P(),
        P(),
    )
    out_specs = (
        P("batch", ("guide", "tensor")),
        P("guide", ("batch", "tensor"), None),
        P("guide", "batch", "tensor"),
    )
    return jax.shard_map(local, mesh=mesh, in_specs=in_specs, out_specs=out_specs, check_vma=False)
```

time: 464 us -> 91.2 us (0.20)
  blocking collectives: 196 us -> 0 us
  waiting for transfers between devices: 178 us -> 0 us
  Pallas kernels: 0 us -> 80.6 us
  matrix products: 27.7 us -> 0 us
  local copies, waits for them, and re-layouts: 24.8 us -> 9.68 us
  between operations: 14.9 us -> 0.64 us
  starting transfers between devices: 12.9 us -> 0 us
  other arithmetic: 8.77 us -> 0 us
    unnamed x4 -> x0, waiting for transfers between devices: 177 us -> none
    pallas_call x0 -> x1, Pallas kernels: none -> 80.6 us  [local(): pl.pallas_call(kernel, name='decode_step', out_shape=(jax.ShapeDtypeStruc...]
    pmax x1 -> x0, blocking collectives: 65 us -> none  [local(): peak = lax.pmax(jnp.max(guided, axis=1), ('guide', 'tensor'))]
    psum x1 -> x0, blocking collectives: 62.9 us -> none  [local(): lax.psum(jnp.sum(jnp.exp(guided - peak[:, None]), axis=1), ('guide', 'ten...]
    all_gather x3 -> x0, blocking collectives: 54.8 us -> none  [the longest x1 20 us: local(): lax.all_gather(rms_norm(own_rows, attn_gain), 'tensor', axis=0, tiled=True)]
    dot_general x9 -> x0, matrix products: 27.7 us -> none  [the longest x1 5.79 us: attend(): jnp.einsum('rkgl,rlkd->rkgd', expd.astype(jnp.bfloat16), values_split, pr...]
    unnamed x23 -> x4, local copies, waits for them, and re-layouts: 23.5 us -> 8.12 us
    all_to_all x1 -> x0, blocking collectives: 12.9 us -> none  [local(): lax.all_to_all(mixed, 'tensor', split_axis=1, concat_axis=0, tiled=True)]
  transfers between devices with their start and end apart: 4 -> 0, of which waited for: 2 -> 0; matrix products, arithmetic and copies ran while one was open for 6% -> 0% of each run, Pallas kernels for 0% -> 0%
where the time goes in v1:
time: 91.2 us; the launch traced here: 90.9 us
  Pallas kernels  80.6 us (88%)
  local copies, waits for them, and re-layouts  9.68 us (11%)
    pallas_call x1, Pallas kernels, local(): pl.pallas_call(kernel, name='decode_step', out_shape=(jax.ShapeDtypeStruc...  80.6 us
    unnamed x4, local copies, waits for them, and re-layouts  8.12 us

profile of v1, /device:TPU:1, one launch (start us, length us, event | category | flops | bytes accessed | tf_op | source)
XLA Modules:
  0.0 90.9 jit_solution(573764082523725201)
XLA Ops:
  0.6 2.2 %copy.20.w_qkv = bf16[2048,192]{1,0:T(8,128)(2,1)} copy(bf16[2048,192]{0,1:T(8,128)(2,1)} %param.19) | data formatting | bytes 1572864 | tf_op args[2]
  2.8 2.2 %copy.21.w_next = bf16[2048,192]{1,0:T(8,128)(2,1)} copy(bf16[2048,192]{0,1:T(8,128)(2,1)} %param.31) | data formatting | bytes 1572864 | tf_op args[14]
  5.1 80.6 %decode_step.1 = (f32[128,2048]{1,0:T(8,128)}, bf16[1,8,2048]{2,1,0:T(8,128)(2,1)}, bf16[1,128,192]{2,1,0:T(8,128)(2,1)}) custom-call(bf16[1,8,2048]{2,1,0:T(8,128)(2,1)} %stream.1, f32[1,2048]{1,0:T(1,128)} %bitcast.4, bf16[2048,192]{1,0:T(8,128)(2,1)} %copy.20.w_qkv, bf16[1,8,1024,512]{3,2,1,0:T(8,128)(2,1)} %keys.1, bf16[1,8,1024,512]{3,2,1,0:T(8,128)(2,1)} %values.1, ...), custom_call_target="tpu_custom_call" | custom-call | tf_op jit(solution)/shard_map/decode_step/pallas_call | solution.py:461
  85.7 1.6 %copy.22 = bf16[1,128,192]{1,2,0:T(8,128)(2,1)} copy(bf16[1,128,192]{2,1,0:T(8,128)(2,1)} %get-tuple-element.5) | data formatting | bytes 98304 | tf_op jit(solution)/shard_map/decode_step/pallas_call | solution.py:461
  87.2 2.3 %copy.25 = f32[128,2048]{1,0:T(8,128)} copy(f32[128,2048]{1,0:T(8,128)} %get-tuple-element.9) | data formatting | bytes 2097152
  89.5 1.4 %copy.26 = bf16[1,8,2048]{2,1,0:T(8,128)(2,1)} copy(bf16[1,8,2048]{2,1,0:T(8,128)(2,1)} %get-tuple-element.10) | data formatting | bytes 65536

commit v2 on v1

v2 whole, which is shorter than its diff:
```python
import functools
import math

import jax
import jax.numpy as jnp
from jax import lax
from jax.experimental import pallas as pl
from jax.experimental.pallas import tpu as pltpu
from jax.sharding import PartitionSpec as P

D = 2048
HEADS = 32
KV_HEADS = 8
GROUPS = HEADS // KV_HEADS
HEAD_DIM = 64
KV_WIDTH = KV_HEADS * HEAD_DIM
TENANTS = 4
SLOTS = 1024
FF_LOCAL = 512
QKV_LOCAL = 192
VOCAB_LOCAL = 2048
ROWS = 128
OWN = 8
SIDE = 4
TENSOR = 16
GUIDE = 2
VOCAB_STEP = 256

EPSILON = 1e-05
ROPE_BASE = 500000.0
MASKED = -1e30
MESH = pl.DeviceIdType.MESH
F32 = jnp.float32
BF16 = jnp.bfloat16
NT = (((1,), (1,)), ((), ()))


def norm_factor(wide):
    return lax.rsqrt(jnp.mean(wide * wide, axis=-1, keepdims=True) + EPSILON)


def rms_norm(wide, gain):
    return wide * norm_factor(wide) * gain


def lane_freq(shape):
    lane = lax.broadcasted_iota(jnp.int32, shape, 1)
    steps_up = (lane % (HEAD_DIM // 2)).astype(F32)
    base_freq = jnp.exp(steps_up * (-2.0 * math.log(ROPE_BASE) / HEAD_DIM))
    wavelen = 2.0 * math.pi / base_freq
    smooth = (8192.0 / wavelen - 1.0) / 3.0
    middle = (1.0 - smooth) * base_freq / 32.0 + smooth * base_freq
    return jnp.where(
        wavelen < 2048.0, base_freq, jnp.where(wavelen > 8192.0, base_freq / 32.0, middle)
    )


def rotate(wide, cosine, sine, first):
    width = wide.shape[-1]
    ahead = pltpu.roll(wide, width - HEAD_DIM // 2, 1)
    behind = pltpu.roll(wide, HEAD_DIM // 2, 1)
    return wide * cosine + jnp.where(first, -ahead, behind) * sine


def spread(block):
    return block.astype(F32).reshape(-1, block.shape[-1]).astype(BF16)


def drain(ref, sem):
    pltpu.make_async_copy(ref, ref, sem).wait()


def send(src, dst, send_sem, recv_sem, device):
    pltpu.make_async_remote_copy(
        src_ref=src,
        dst_ref=dst,
        send_sem=send_sem,
        recv_sem=recv_sem,
        device_id=device,
        device_id_type=MESH,
    ).start()


def distance(step):
    return min(step, SIDE - step)


OFFSETS = sorted(
    ((dy, dx) for dy in range(SIDE) for dx in range(SIDE)),
    key=lambda at: -distance(at[0]) - distance(at[1]),
)


def kernel(
    stream, attn_gain, w_qkv, keys, values, lengths, w_out, mlp_gain, w_gate, w_up, w_down,
    final_gain, lm_head, next_gain, w_next, counts, levels,
    guided_all, level_out, layer_out, next_qkv,
    stream_v, gains_v, w_qkv_v, keys_v, values_v, w_out_v, w_gate_v, w_up_v, w_down_v, lm_head_v, w_next_v,
    stream_all, proj, request_side, queries, mixed, head_out, head_all, w_cols, after_own, after_all, after_rows,
    partial, shares, layer_own, layer_all, layer_other, final_rows, next_rows, stats_own, stats_all,
    load_sems, sends, recvs,
):
    guide = lax.axis_index("guide")
    me = lax.axis_index("tensor")
    batch = lax.axis_index("batch")
    y = me // SIDE
    x = lax.rem(me, SIDE)
    other = 1 - guide
    chips = [lax.rem(y + dy, SIDE) * SIDE + lax.rem(x + dx, SIDE) for dy, dx in OFFSETS]

    barrier = pltpu.get_barrier_semaphore()
    for there in chips:
        pl.semaphore_signal(
            barrier, inc=1, device_id={"guide": other, "tensor": there}, device_id_type=MESH
        )
    for there in chips[:-1]:
        pl.semaphore_signal(barrier, inc=1, device_id={"tensor": there}, device_id_type=MESH)

    loads = [
        pltpu.make_async_copy(stream.at[0], stream_v, load_sems.at[0]),
        pltpu.make_async_copy(attn_gain, gains_v.at[0], load_sems.at[1]),
        pltpu.make_async_copy(w_qkv, w_qkv_v, load_sems.at[2]),
        pltpu.make_async_copy(w_out, w_out_v, load_sems.at[3]),
        pltpu.make_async_copy(keys.at[0], keys_v, load_sems.at[4]),
        pltpu.make_async_copy(values.at[0], values_v, load_sems.at[5]),
        pltpu.make_async_copy(mlp_gain, gains_v.at[1], load_sems.at[6]),
        pltpu.make_async_copy(w_gate, w_gate_v, load_sems.at[7]),
        pltpu.make_async_copy(w_up, w_up_v, load_sems.at[8]),
        pltpu.make_async_copy(w_down, w_down_v, load_sems.at[9]),
        pltpu.make_async_copy(next_gain, gains_v.at[2], load_sems.at[10]),
        pltpu.make_async_copy(final_gain, gains_v.at[3], load_sems.at[11]),
        pltpu.make_async_copy(w_next, w_next_v, load_sems.at[12]),
        pltpu.make_async_copy(lm_head, lm_head_v, load_sems.at[13]),
    ]
    for load in loads:
        load.start()
    left = dict(enumerate(loads))
    finish = []

    def ready(*which):
        for k in which:
            left.pop(k).wait()

    def cross(phase, part, dst, whole):
        for there in chips:
            send(part(there), dst, sends.at[phase], recvs.at[phase], {"guide": other, "tensor": there})
        finish.append(lambda: drain(whole, sends.at[phase]))

    pl.semaphore_wait(barrier, 2 * TENSOR - 1)
    ready(0)
    cross(0, lambda there: stream_v, stream_all.at[me], stream_all)

    row = lax.broadcasted_iota(jnp.int32, (OWN, 2 * HEAD_DIM), 0)
    position = jnp.zeros((OWN, 2 * HEAD_DIM), F32)
    for r in range(OWN):
        position = jnp.where(row == r, lengths[0, r].astype(F32), position)
    angle = position * lane_freq((OWN, 2 * HEAD_DIM))
    cosine = jnp.concatenate([jnp.cos(angle)] * (KV_WIDTH // (2 * HEAD_DIM)), axis=1)
    sine = jnp.concatenate([jnp.sin(angle)] * (KV_WIDTH // (2 * HEAD_DIM)), axis=1)
    ready(1, 2, 3)
    drain(stream_all, recvs.at[0])

    wide = stream_all[...].astype(F32).reshape(ROWS, D)
    rows = rms_norm(wide, gains_v[0]).astype(BF16)
    projected = lax.dot_general(rows, w_qkv_v[...], NT, preferred_element_type=F32)
    proj[:, :, 0:QKV_LOCAL] = projected.reshape(TENSOR, OWN, QKV_LOCAL).astype(BF16)
    cross(1, lambda there: proj.at[there], request_side.at[me], request_side)
    drain(request_side, recvs.at[1])
    cross(
        2,
        lambda there: w_out_v.at[:, pl.ds(pl.multiple_of(there * ROWS, ROWS), ROWS)],
        w_cols.at[me],
        w_cols,
    )

    def piece(column):
        at, j = divmod(column, 3)
        return request_side[at, :, j * HEAD_DIM : (j + 1) * HEAD_DIM].astype(F32)

    lane = lax.broadcasted_iota(jnp.int32, (OWN, KV_WIDTH), 1)
    first = lax.rem(lane, HEAD_DIM) < HEAD_DIM // 2
    for g in range(GROUPS):
        wide = jnp.concatenate([piece(GROUPS * k + g) for k in range(KV_HEADS)], axis=1)
        queries[g] = rotate(wide, cosine, sine, first).astype(BF16).astype(F32) * (HEAD_DIM**-0.5)
    wide = jnp.concatenate([piece(HEADS + k) for k in range(KV_HEADS)], axis=1)
    queries[GROUPS] = rotate(wide, cosine, sine, first).astype(BF16).astype(F32)
    queries[GROUPS + 1] = jnp.concatenate(
        [piece(HEADS + KV_HEADS + k) for k in range(KV_HEADS)], axis=1
    )

    ready(4, 5)
    own_head = lane // HEAD_DIM == lax.broadcasted_iota(jnp.int32, (OWN, KV_WIDTH), 0)
    slot = lax.broadcasted_iota(jnp.int32, (HEADS, SLOTS), 1)

    def attend(r, carry):
        rowed = [
            jnp.where(own_head, jnp.broadcast_to(queries[g, pl.ds(r, 1), :], (KV_HEADS, KV_WIDTH)), 0.0)
            for g in range(GROUPS)
        ]
        spread_q = jnp.concatenate(rowed, axis=0)
        new_key = queries[GROUPS, pl.ds(r, 1), :]
        new_value = queries[GROUPS + 1, pl.ds(r, 1), :]
        scores = lax.dot_general(spread_q.astype(BF16), keys_v[r], NT, preferred_element_type=F32)
        fresh = jnp.sum(spread_q * new_key, axis=1, keepdims=True)
        scores = jnp.where(slot < lengths[0, r], scores, MASKED)
        peak = jnp.maximum(jnp.max(scores, axis=1, keepdims=True), fresh)
        expd = jnp.exp(scores - peak)
        fresh_exp = jnp.exp(fresh - peak)
        total = jnp.sum(expd, axis=1, keepdims=True) + fresh_exp
        weighted = jnp.dot(expd.astype(BF16), values_v[r], preferred_element_type=F32)
        weighted = weighted + fresh_exp.astype(BF16).astype(F32) * new_value
        weighted = weighted / total
        for g in range(GROUPS):
            kept = jnp.where(own_head, weighted[g * KV_HEADS : (g + 1) * KV_HEADS], 0.0)
            mixed[g, pl.ds(r, 1), :] = jnp.sum(kept, axis=0, keepdims=True)
        return carry

    lax.fori_loop(0, OWN, attend, 0, unroll=True)
    for k in range(KV_HEADS):
        here = slice(k * HEAD_DIM, (k + 1) * HEAD_DIM)
        head_out[:, k * GROUPS * HEAD_DIM : (k + 1) * GROUPS * HEAD_DIM] = jnp.concatenate(
            [mixed[g, :, here] for g in range(GROUPS)], axis=1
        ).astype(BF16)
    cross(3, lambda there: head_out, head_all.at[me], head_all)
    drain(w_cols, recvs.at[2])
    drain(head_all, recvs.at[3])

    terms = jnp.dot(
        spread(head_all[...]), w_cols[...].reshape(D, ROWS), preferred_element_type=F32
    )
    wide = stream_all[:, :, pl.ds(pl.multiple_of(me * ROWS, ROWS), ROWS)].astype(F32)
    after_own[...] = (wide + terms.reshape(TENSOR, OWN, ROWS)).astype(BF16)
    cross(4, lambda there: after_own, after_all.at[me], after_all)
    ready(6, 7, 8, 9)
    drain(after_all, recvs.at[4])
    own = after_all.at[:, me]
    send(own, after_rows, sends.at[8], recvs.at[8], {"guide": other})
    finish.append(lambda: drain(after_rows, sends.at[8]))

    wide = jnp.concatenate(
        [after_all[k].astype(F32).reshape(ROWS, ROWS) for k in range(TENSOR)], axis=1
    )
    rows = rms_norm(wide, gains_v[1]).astype(BF16)
    gate = jnp.dot(rows, w_gate_v[...], preferred_element_type=F32)
    upward = jnp.dot(rows, w_up_v[...], preferred_element_type=F32)
    hidden = (gate * jax.nn.sigmoid(gate) * upward).astype(BF16)
    terms = jnp.dot(hidden, w_down_v[...], preferred_element_type=F32)
    partial[...] = terms.reshape(TENSOR, OWN, D).astype(BF16)
    cross(5, lambda there: partial.at[there], shares.at[me], shares)
    drain(after_rows, recvs.at[8])
    wide = jnp.concatenate([after_rows[k].astype(F32) for k in range(TENSOR)], axis=1)
    drain(shares, recvs.at[5])
    share = shares[0].astype(F32)
    for k in range(1, TENSOR):
        share = share + shares[k].astype(F32)
    layer_own[...] = (wide + share).astype(BF16)
    cross(6, lambda there: layer_own, layer_all.at[me], layer_all)

    request = batch * ROWS + lax.broadcasted_iota(jnp.int32, (ROWS, VOCAB_STEP), 0)
    level = jnp.full((ROWS, VOCAB_STEP), levels[0].astype(F32))
    bound = counts[0]
    for t in range(1, TENANTS):
        level = jnp.where(request >= bound, levels[t].astype(F32), level)
        bound = bound + counts[t]
    weight = level * 0.25
    ready(10, 11, 12, 13)
    drain(layer_all, recvs.at[6])
    send(layer_all, layer_other, sends.at[9], recvs.at[9], {"guide": other})
    finish.append(lambda: drain(layer_other, sends.at[9]))
    layer_out[...] = layer_all[me]

    def norm_own(at, carry):
        wide = layer_all[pl.ds(at * SIDE, SIDE)].astype(F32).reshape(SIDE * OWN, D)
        scaled = wide * norm_factor(wide)
        start = pl.multiple_of(at * SIDE * OWN, SIDE * OWN)
        next_rows[pl.ds(start, SIDE * OWN), :] = (scaled * gains_v[2]).astype(BF16)
        final_rows[guide, pl.ds(start, SIDE * OWN), :] = (scaled * gains_v[3]).astype(BF16)
        return carry

    lax.fori_loop(0, SIDE, norm_own, 0)
    drain(layer_other, recvs.at[9])

    def norm_other(at, carry):
        wide = layer_other[pl.ds(at * SIDE, SIDE)].astype(F32).reshape(SIDE * OWN, D)
        start = pl.multiple_of(at * SIDE * OWN, SIDE * OWN)
        final_rows[other, pl.ds(start, SIDE * OWN), :] = rms_norm(wide, gains_v[3]).astype(BF16)
        return carry

    lax.fori_loop(0, SIDE, norm_other, 0)

    def score(step, top):
        start = pl.multiple_of(step * VOCAB_STEP, VOCAB_STEP)
        logits = lax.dot_general(
            final_rows[...].reshape(GUIDE * ROWS, D), lm_head_v[pl.ds(start, VOCAB_STEP), :], NT,
            preferred_element_type=F32,
        )
        uncond = logits[ROWS:]
        guided = uncond + weight * (logits[:ROWS] - uncond)
        guided_all[:, pl.ds(start, VOCAB_STEP)] = guided
        return jnp.maximum(top, guided)

    top = lax.fori_loop(
        0, VOCAB_LOCAL // VOCAB_STEP, score, jnp.full((ROWS, VOCAB_STEP), -jnp.inf, F32)
    )
    top = jnp.max(top, axis=1, keepdims=True)

    def add_up(step, total):
        start = pl.multiple_of(step * VOCAB_STEP, VOCAB_STEP)
        return total + jnp.exp(guided_all[:, pl.ds(start, VOCAB_STEP)] - top)

    mass = lax.fori_loop(
        0, VOCAB_LOCAL // VOCAB_STEP, add_up, jnp.zeros((ROWS, VOCAB_STEP), F32)
    )
    mass = jnp.sum(mass, axis=1, keepdims=True)
    column = lax.broadcasted_iota(jnp.int32, (ROWS, ROWS), 1)
    packed = jnp.where(column == 0, top, mass)
    place = guide * TENSOR + me
    mine = jnp.transpose(packed)[0:8]
    stats_own[...] = mine
    stats_all[place] = mine
    for there in chips:
        send(stats_own, stats_all.at[place], sends.at[7], recvs.at[7], {"guide": other, "tensor": there})
    for there in chips[:-1]:
        send(stats_own, stats_all.at[place], sends.at[7], recvs.at[7], {"tensor": there})
    finish.append(lambda: drain(stats_all.at[pl.ds(0, GUIDE * TENSOR - 1)], sends.at[7]))
    next_qkv[...] = lax.dot_general(
        w_next_v[...], next_rows[...], NT, preferred_element_type=F32
    ).astype(BF16)
    drain(stats_all.at[pl.ds(0, GUIDE * TENSOR - 1)], recvs.at[7])
    peaks = stats_all[:, 0, :]
    peak = jnp.max(peaks, axis=0, keepdims=True)
    total = jnp.sum(stats_all[:, 1, :] * jnp.exp(peaks - peak), axis=0, keepdims=True)
    level_out[...] = jnp.transpose(jnp.broadcast_to(peak + jnp.log(total), (ROWS, ROWS)))

    for last in finish:
        last()


def settle(guided, level, layer_rows, next_rows, logprobs, layer_out, next_qkv):
    layer_out[...] = layer_rows[...]
    next_qkv[...] = next_rows[...]
    wide = jnp.concatenate([level[...]] * (VOCAB_LOCAL // ROWS), axis=1)
    logprobs[...] = guided[...] - wide


def local(
    stream, attn_gain, w_qkv, cache_keys, cache_values, cache_len, w_out, mlp_gain, w_gate, w_up, w_down,
    final_gain, lm_head, next_gain, w_next, tenant_counts, guide_level,
):
    hbm = pl.BlockSpec(memory_space=pl.ANY)
    smem = pl.BlockSpec(memory_space=pltpu.SMEM)
    vmem = pl.BlockSpec(memory_space=pltpu.VMEM)
    dma = pltpu.SemaphoreType.DMA
    wide = lambda gain: gain.reshape(1, D)
    guided, level, layer_rows, next_rows = pl.pallas_call(
        kernel,
        name="decode_step",
        out_shape=(
            jax.ShapeDtypeStruct((ROWS, VOCAB_LOCAL), F32),
            jax.ShapeDtypeStruct((ROWS, ROWS), F32),
            jax.ShapeDtypeStruct((OWN, D), BF16),
            jax.ShapeDtypeStruct((QKV_LOCAL, ROWS), BF16),
        ),
        in_specs=[hbm] * 5 + [smem] + [hbm] * 9 + [smem] * 2,
        out_specs=(vmem, vmem, vmem, vmem),
        scratch_shapes=[
            pltpu.VMEM((OWN, D), BF16),
            pltpu.VMEM((4, 1, D), F32),
            pltpu.VMEM((QKV_LOCAL, D), BF16),
            pltpu.VMEM((OWN, SLOTS, KV_WIDTH), BF16),
            pltpu.VMEM((OWN, SLOTS, KV_WIDTH), BF16),
            pltpu.VMEM((ROWS, D), BF16),
            pltpu.VMEM((D, FF_LOCAL), BF16),
            pltpu.VMEM((D, FF_LOCAL), BF16),
            pltpu.VMEM((FF_LOCAL, D), BF16),
            pltpu.VMEM((VOCAB_LOCAL, D), BF16),
            pltpu.VMEM((QKV_LOCAL, D), BF16),
            pltpu.VMEM((TENSOR, OWN, D), BF16),
            pltpu.VMEM((TENSOR, OWN, QKV_LOCAL), BF16),
            pltpu.VMEM((TENSOR, OWN, QKV_LOCAL), BF16),
            pltpu.VMEM((GROUPS + 2, OWN, KV_WIDTH), F32),
            pltpu.VMEM((GROUPS, OWN, KV_WIDTH), F32),
            pltpu.VMEM((OWN, D), BF16),
            pltpu.VMEM((TENSOR, OWN, D), BF16),
            pltpu.VMEM((TENSOR, ROWS, ROWS), BF16),
            pltpu.VMEM((TENSOR, OWN, ROWS), BF16),
            pltpu.VMEM((TENSOR, TENSOR, OWN, ROWS), BF16),
            pltpu.VMEM((TENSOR, OWN, ROWS), BF16),
            pltpu.VMEM((TENSOR, OWN, D), BF16),
            pltpu.VMEM((TENSOR, OWN, D), BF16),
            pltpu.VMEM((OWN, D), BF16),
            pltpu.VMEM((TENSOR, OWN, D), BF16),
            pltpu.VMEM((TENSOR, OWN, D), BF16),
            pltpu.VMEM((GUIDE, ROWS, D), BF16),
            pltpu.VMEM((ROWS, D), BF16),
            pltpu.VMEM((8, ROWS), F32),
            pltpu.VMEM((GUIDE * TENSOR, 8, ROWS), F32),
            dma((14,)),
            dma((10,)),
            dma((10,)),
        ],
        compiler_params=pltpu.CompilerParams(
            collective_id=0, has_side_effects=True, vmem_limit_bytes=60 * 1024 * 1024
        ),
    )(
        stream, wide(attn_gain), w_qkv.T, cache_keys, cache_values, cache_len, w_out, wide(mlp_gain),
        w_gate, w_up, w_down, wide(final_gain), lm_head, wide(next_gain), w_next.T, tenant_counts, guide_level,
    )

    logprobs, layer_out, next_qkv = pl.pallas_call(
        settle,
        name="settle",
        out_shape=(
            jax.ShapeDtypeStruct((ROWS, VOCAB_LOCAL), F32),
            jax.ShapeDtypeStruct((OWN, D), BF16),
            jax.ShapeDtypeStruct((QKV_LOCAL, ROWS), BF16),
        ),
        in_specs=[vmem] * 4,
        out_specs=(vmem, vmem, vmem),
    )(guided, level, layer_rows, next_rows)
    return logprobs, layer_out[None], next_qkv.T[None]


def solution(mesh):
    in_specs = (
        P("guide", ("batch", "tensor"), None),
        P(),
        P(None, "tensor"),
        P("guide", ("batch", "tensor"), None, None),
        P("guide", ("batch", "tensor"), None, None),
        P("guide", ("batch", "tensor")),
        P("tensor", None),
        P(),
        P(None, "tensor"),
        P(None, "tensor"),
        P("tensor", None),
        P(),
        P(("guide", "tensor"), None),
        P(),
        P(None, "tensor"),
        P(),
        P(),
    )
    out_specs = (
        P("batch", ("guide", "tensor")),
        P("guide", ("batch", "tensor"), None),
        P("guide", "batch", "tensor"),
    )
    return jax.shard_map(local, mesh=mesh, in_specs=in_specs, out_specs=out_specs, check_vma=False)
```

time: 91.2 us -> 76.5 us (0.84)
  local copies, waits for them, and re-layouts: 9.68 us -> 0 us
  Pallas kernels: 80.6 us -> 75.7 us
    unnamed x4 -> x0, local copies, waits for them, and re-layouts: 8.12 us -> none
    pallas_call x1, Pallas kernels: 80.6 us -> 73.4 us  [local(): pl.pallas_call(kernel, name='decode_step', out_shape=(jax.ShapeDtypeStruc...]
    pallas_call x0 -> x1, Pallas kernels: none -> 2.32 us  [local(): pl.pallas_call(settle, name='settle', out_shape=(jax.ShapeDtypeStruct((RO...]
    pallas_call x1 -> x0, local copies, waits for them, and re-layouts: 1.56 us -> none  [local(): pl.pallas_call(kernel, name='decode_step', out_shape=(jax.ShapeDtypeStruc...]
where the time goes in v2:
time: 76.5 us; the launch traced here: 76.4 us
  Pallas kernels  75.7 us (99%)
    pallas_call x1, Pallas kernels, local(): pl.pallas_call(kernel, name='decode_step', out_shape=(jax.ShapeDtypeStruc...  73.4 us
    pallas_call x1, Pallas kernels, local(): pl.pallas_call(settle, name='settle', out_shape=(jax.ShapeDtypeStruct((RO...  2.32 us

profile of v2, /device:TPU:1, one launch (start us, length us, event | category | flops | bytes accessed | tf_op | source)
XLA Modules:
  0.0 76.4 jit_solution(18106138836456848430)
XLA Ops:
  0.6 73.4 %decode_step.1 = (f32[128,2048]{1,0:T(8,128)}, f32[128,128]{1,0:T(8,128)}, bf16[8,2048]{1,0:T(8,128)(2,1)}, bf16[192,128]{1,0:T(8,128)(2,1)}) custom-call(bf16[1,8,2048]{2,1,0:T(8,128)(2,1)} %stream.1, f32[1,2048]{1,0:T(1,128)} %bitcast.12, bf16[192,2048]{1,0:T(8,128)(2,1)} %bitcast.10, bf16[1,8,1024,512]{3,2,1,0:T(8,128)(2,1)} %keys.1, ...), custom_call_target="tpu_custom_call" | custom-call | tf_op jit(solution)/shard_map/decode_step/pallas_call | solution.py:355
  74.0 2.3 %settle.1 = (f32[128,2048]{1,0:T(8,128)}, bf16[8,2048]{1,0:T(8,128)(2,1)}, bf16[192,128]{1,0:T(8,128)(2,1)}) custom-call(f32[128,2048]{1,0:T(8,128)} %get-tuple-element.10.guided, f32[128,128]{1,0:T(8,128)} %get-tuple-element.11.level, bf16[8,2048]{1,0:T(8,128)(2,1)} %get-tuple-element.12.layer_rows, bf16[192,128]{1,0:T(8,128)(2,1)} %get-tuple-element.13.next_rows), custom_call_target="tpu_custom_call" | custom-call | tf_op jit(solution)/shard_map/settle/pallas_call | solution.py:410

commit v3 on v2

--- a/solution.py
+++ b/solution.py
@@ -96,8 +96,8 @@
     final_gain, lm_head, next_gain, w_next, counts, levels,
     guided_all, level_out, layer_out, next_qkv,
     stream_v, gains_v, w_qkv_v, keys_v, values_v, w_out_v, w_gate_v, w_up_v, w_down_v, lm_head_v, w_next_v,
-    stream_all, proj, request_side, queries, mixed, head_out, head_all, w_cols, after_own, after_all, after_rows,
-    partial, shares, layer_own, layer_all, layer_other, final_rows, next_rows, stats_own, stats_all,
+    stream_all, proj, request_side, queries, scores, probs, mixed, head_out, head_all, w_cols, after_own, after_all, after_rows,
+    partial, shares, layer_own, layer_all, final_rows, cond_all, stats_own, stats_all,
     load_sems, sends, recvs,
 ):
     guide = lax.axis_index("guide")
@@ -141,14 +141,17 @@
         for k in which:
             left.pop(k).wait()
 
-    def cross(phase, part, dst, whole):
-        for there in chips:
-            send(part(there), dst, sends.at[phase], recvs.at[phase], {"guide": other, "tensor": there})
+    def cross(phase, part, dst, whole, early=None):
+        for offset, there in zip(OFFSETS, chips):
+            landed = recvs.at[10] if offset == early else recvs.at[phase]
+            send(part(there), dst, sends.at[phase], landed, {"guide": other, "tensor": there})
         finish.append(lambda: drain(whole, sends.at[phase]))
 
     pl.semaphore_wait(barrier, 2 * TENSOR - 1)
     ready(0)
-    cross(0, lambda there: stream_v, stream_all.at[me], stream_all)
+    pl.when(guide == 1)(lambda: drain(stream_all.at[0], recvs.at[10]))
+    cross(0, lambda there: stream_v, stream_all.at[me], stream_all, early=(0, 1))
+    pl.when(guide == 0)(lambda: drain(stream_all.at[0], recvs.at[10]))
 
     row = lax.broadcasted_iota(jnp.int32, (OWN, 2 * HEAD_DIM), 0)
     position = jnp.zeros((OWN, 2 * HEAD_DIM), F32)
@@ -158,20 +161,22 @@
     cosine = jnp.concatenate([jnp.cos(angle)] * (KV_WIDTH // (2 * HEAD_DIM)), axis=1)
     sine = jnp.concatenate([jnp.sin(angle)] * (KV_WIDTH // (2 * HEAD_DIM)), axis=1)
     ready(1, 2, 3)
-    drain(stream_all, recvs.at[0])
+    drain(stream_all.at[pl.ds(0, TENSOR - 1)], recvs.at[0])
 
     wide = stream_all[...].astype(F32).reshape(ROWS, D)
     rows = rms_norm(wide, gains_v[0]).astype(BF16)
     projected = lax.dot_general(rows, w_qkv_v[...], NT, preferred_element_type=F32)
     proj[:, :, 0:QKV_LOCAL] = projected.reshape(TENSOR, OWN, QKV_LOCAL).astype(BF16)
     cross(1, lambda there: proj.at[there], request_side.at[me], request_side)
-    drain(request_side, recvs.at[1])
+    half = pl.ds(pl.multiple_of(guide * (ROWS // 2), ROWS // 2), ROWS // 2)
+    rest = pl.ds(pl.multiple_of(other * (ROWS // 2), ROWS // 2), ROWS // 2)
     cross(
         2,
-        lambda there: w_out_v.at[:, pl.ds(pl.multiple_of(there * ROWS, ROWS), ROWS)],
-        w_cols.at[me],
-        w_cols,
-    )
+        lambda there: w_out_v.at[half, pl.ds(pl.multiple_of(there * ROWS, ROWS), ROWS)],
+        w_cols.at[me, half],
+        w_cols.at[:, half],
+    )
+    drain(request_side, recvs.at[1])
 
     def piece(column):
         at, j = divmod(column, 3)
@@ -192,37 +197,42 @@
     own_head = lane // HEAD_DIM == lax.broadcasted_iota(jnp.int32, (OWN, KV_WIDTH), 0)
     slot = lax.broadcasted_iota(jnp.int32, (HEADS, SLOTS), 1)
 
-    def attend(r, carry):
-        rowed = [
-            jnp.where(own_head, jnp.broadcast_to(queries[g, pl.ds(r, 1), :], (KV_HEADS, KV_WIDTH)), 0.0)
-            for g in range(GROUPS)
-        ]
-        spread_q = jnp.concatenate(rowed, axis=0)
-        new_key = queries[GROUPS, pl.ds(r, 1), :]
-        new_value = queries[GROUPS + 1, pl.ds(r, 1), :]
-        scores = lax.dot_general(spread_q.astype(BF16), keys_v[r], NT, preferred_element_type=F32)
-        fresh = jnp.sum(spread_q * new_key, axis=1, keepdims=True)
-        scores = jnp.where(slot < lengths[0, r], scores, MASKED)
-        peak = jnp.maximum(jnp.max(scores, axis=1, keepdims=True), fresh)
-        expd = jnp.exp(scores - peak)
-        fresh_exp = jnp.exp(fresh - peak)
-        total = jnp.sum(expd, axis=1, keepdims=True) + fresh_exp
-        weighted = jnp.dot(expd.astype(BF16), values_v[r], preferred_element_type=F32)
-        weighted = weighted + fresh_exp.astype(BF16).astype(F32) * new_value
-        weighted = weighted / total
+    fresh = []
+    for r in range(OWN):
+        spread_q = jnp.concatenate(
+            [
+                jnp.where(own_head, jnp.broadcast_to(queries[g, r : r + 1, :], (KV_HEADS, KV_WIDTH)), 0.0)
+                for g in range(GROUPS)
+            ],
+            axis=0,
+        )
+        scores[r] = lax.dot_general(spread_q.astype(BF16), keys_v[r], NT, preferred_element_type=F32)
+        fresh.append(jnp.sum(spread_q * queries[GROUPS, r : r + 1, :], axis=1, keepdims=True))
+    drain(w_cols.at[:, rest], recvs.at[2])
+    send(w_cols.at[:, rest], w_cols.at[:, rest], sends.at[11], recvs.at[11], {"guide": other})
+    finish.append(lambda: drain(w_cols.at[:, rest], sends.at[11]))
+    totals = []
+    for r in range(OWN):
+        masked = jnp.where(slot < lengths[0, r], scores[r], MASKED)
+        peak = jnp.maximum(jnp.max(masked, axis=1, keepdims=True), fresh[r])
+        expd = jnp.exp(masked - peak)
+        fresh[r] = jnp.exp(fresh[r] - peak)
+        totals.append(jnp.sum(expd, axis=1, keepdims=True) + fresh[r])
+        probs[r] = expd.astype(BF16)
+    for r in range(OWN):
+        weighted = jnp.dot(probs[r], values_v[r], preferred_element_type=F32)
+        weighted = weighted + fresh[r].astype(BF16).astype(F32) * queries[GROUPS + 1, r : r + 1, :]
+        weighted = weighted / totals[r]
         for g in range(GROUPS):
             kept = jnp.where(own_head, weighted[g * KV_HEADS : (g + 1) * KV_HEADS], 0.0)
-            mixed[g, pl.ds(r, 1), :] = jnp.sum(kept, axis=0, keepdims=True)
-        return carry
-
-    lax.fori_loop(0, OWN, attend, 0, unroll=True)
+            mixed[g, r : r + 1, :] = jnp.sum(kept, axis=0, keepdims=True)
     for k in range(KV_HEADS):
         here = slice(k * HEAD_DIM, (k + 1) * HEAD_DIM)
         head_out[:, k * GROUPS * HEAD_DIM : (k + 1) * GROUPS * HEAD_DIM] = jnp.concatenate(
             [mixed[g, :, here] for g in range(GROUPS)], axis=1
         ).astype(BF16)
     cross(3, lambda there: head_out, head_all.at[me], head_all)
-    drain(w_cols, recvs.at[2])
+    drain(w_cols.at[:, half], recvs.at[11])
     drain(head_all, recvs.at[3])
 
     terms = jnp.dot(
@@ -254,7 +264,7 @@
     for k in range(1, TENSOR):
         share = share + shares[k].astype(F32)
     layer_own[...] = (wide + share).astype(BF16)
-    cross(6, lambda there: layer_own, layer_all.at[me], layer_all)
+    cross(6, lambda there: layer_own, layer_all.at[other, me], layer_all.at[other])
 
     request = batch * ROWS + lax.broadcasted_iota(jnp.int32, (ROWS, VOCAB_STEP), 0)
     level = jnp.full((ROWS, VOCAB_STEP), levels[0].astype(F32))
@@ -264,53 +274,44 @@
         bound = bound + counts[t]
     weight = level * 0.25
     ready(10, 11, 12, 13)
-    drain(layer_all, recvs.at[6])
-    send(layer_all, layer_other, sends.at[9], recvs.at[9], {"guide": other})
-    finish.append(lambda: drain(layer_other, sends.at[9]))
-    layer_out[...] = layer_all[me]
-
-    def norm_own(at, carry):
-        wide = layer_all[pl.ds(at * SIDE, SIDE)].astype(F32).reshape(SIDE * OWN, D)
-        scaled = wide * norm_factor(wide)
-        start = pl.multiple_of(at * SIDE * OWN, SIDE * OWN)
-        next_rows[pl.ds(start, SIDE * OWN), :] = (scaled * gains_v[2]).astype(BF16)
-        final_rows[guide, pl.ds(start, SIDE * OWN), :] = (scaled * gains_v[3]).astype(BF16)
-        return carry
-
-    lax.fori_loop(0, SIDE, norm_own, 0)
-    drain(layer_other, recvs.at[9])
-
-    def norm_other(at, carry):
-        wide = layer_other[pl.ds(at * SIDE, SIDE)].astype(F32).reshape(SIDE * OWN, D)
-        start = pl.multiple_of(at * SIDE * OWN, SIDE * OWN)
-        final_rows[other, pl.ds(start, SIDE * OWN), :] = rms_norm(wide, gains_v[3]).astype(BF16)
-        return carry
-
-    lax.fori_loop(0, SIDE, norm_other, 0)
-
-    def score(step, top):
-        start = pl.multiple_of(step * VOCAB_STEP, VOCAB_STEP)
-        logits = lax.dot_general(
-            final_rows[...].reshape(GUIDE * ROWS, D), lm_head_v[pl.ds(start, VOCAB_STEP), :], NT,
+
+    def arrive(branch):
+        @pl.when(guide == branch)
+        def _():
+            drain(layer_all.at[branch], recvs.at[6])
+            send(layer_all.at[branch], layer_all.at[branch], sends.at[9], recvs.at[9], {"guide": other})
+
+        pl.when(guide != branch)(lambda: drain(layer_all.at[branch], recvs.at[9]))
+        for at in range(0, TENSOR, SIDE):
+            wide = layer_all[branch, at : at + SIDE].astype(F32).reshape(SIDE * OWN, D)
+            final_rows[at * OWN : (at + SIDE) * OWN] = rms_norm(wide, gains_v[3]).astype(BF16)
+
+    def logits(step):
+        return lax.dot_general(
+            final_rows[...], lm_head_v[step * VOCAB_STEP : (step + 1) * VOCAB_STEP], NT,
             preferred_element_type=F32,
         )
-        uncond = logits[ROWS:]
-        guided = uncond + weight * (logits[:ROWS] - uncond)
-        guided_all[:, pl.ds(start, VOCAB_STEP)] = guided
-        return jnp.maximum(top, guided)
-
-    top = lax.fori_loop(
-        0, VOCAB_LOCAL // VOCAB_STEP, score, jnp.full((ROWS, VOCAB_STEP), -jnp.inf, F32)
-    )
+
+    steps = VOCAB_LOCAL // VOCAB_STEP
+    arrive(0)
+    for step in range(steps):
+        cond_all[:, step * VOCAB_STEP : (step + 1) * VOCAB_STEP] = logits(step)
+    arrive(1)
+    finish.append(lambda: drain(layer_all.at[0], sends.at[9]))
+    top = jnp.full((ROWS, VOCAB_STEP), -jnp.inf, F32)
+    for step in range(steps):
+        here = slice(step * VOCAB_STEP, (step + 1) * VOCAB_STEP)
+        uncond = logits(step)
+        guided = uncond + weight * (cond_all[:, here] - uncond)
+        cond_all[:, here] = guided
+        top = jnp.maximum(top, guided)
+        copy = pltpu.make_async_copy(cond_all.at[:, here], guided_all.at[:, here], load_sems.at[step])
+        copy.start()
+        finish.append(copy.wait)
     top = jnp.max(top, axis=1, keepdims=True)
-
-    def add_up(step, total):
-        start = pl.multiple_of(step * VOCAB_STEP, VOCAB_STEP)
-        return total + jnp.exp(guided_all[:, pl.ds(start, VOCAB_STEP)] - top)
-
-    mass = lax.fori_loop(
-        0, VOCAB_LOCAL // VOCAB_STEP, add_up, jnp.zeros((ROWS, VOCAB_STEP), F32)
-    )
+    mass = jnp.zeros((ROWS, VOCAB_STEP), F32)
+    for step in range(steps):
+        mass = mass + jnp.exp(cond_all[:, step * VOCAB_STEP : (step + 1) * VOCAB_STEP] - top)
     mass = jnp.sum(mass, axis=1, keepdims=True)
     column = lax.broadcasted_iota(jnp.int32, (ROWS, ROWS), 1)
     packed = jnp.where(column == 0, top, mass)
@@ -323,8 +324,13 @@
     for there in chips[:-1]:
         send(stats_own, stats_all.at[place], sends.at[7], recvs.at[7], {"tensor": there})
     finish.append(lambda: drain(stats_all.at[pl.ds(0, GUIDE * TENSOR - 1)], sends.at[7]))
+
+    layer_out[...] = layer_all[guide, me]
+    for at in range(0, TENSOR, SIDE):
+        wide = layer_all[guide, pl.ds(at, SIDE)].astype(F32).reshape(SIDE * OWN, D)
+        final_rows[at * OWN : (at + SIDE) * OWN] = rms_norm(wide, gains_v[2]).astype(BF16)
     next_qkv[...] = lax.dot_general(
-        w_next_v[...], next_rows[...], NT, preferred_element_type=F32
+        w_next_v[...], final_rows[...], NT, preferred_element_type=F32
     ).astype(BF16)
     drain(stats_all.at[pl.ds(0, GUIDE * TENSOR - 1)], recvs.at[7])
     peaks = stats_all[:, 0, :]
@@ -362,7 +368,7 @@
             jax.ShapeDtypeStruct((QKV_LOCAL, ROWS), BF16),
         ),
         in_specs=[hbm] * 5 + [smem] + [hbm] * 9 + [smem] * 2,
-        out_specs=(vmem, vmem, vmem, vmem),
+        out_specs=(hbm, vmem, vmem, vmem),
         scratch_shapes=[
             pltpu.VMEM((OWN, D), BF16),
             pltpu.VMEM((4, 1, D), F32),
@@ -379,6 +385,8 @@
             pltpu.VMEM((TENSOR, OWN, QKV_LOCAL), BF16),
             pltpu.VMEM((TENSOR, OWN, QKV_LOCAL), BF16),
             pltpu.VMEM((GROUPS + 2, OWN, KV_WIDTH), F32),
+            pltpu.VMEM((OWN, HEADS, SLOTS), F32),
+            pltpu.VMEM((OWN, HEADS, SLOTS), BF16),
             pltpu.VMEM((GROUPS, OWN, KV_WIDTH), F32),
             pltpu.VMEM((OWN, D), BF16),
             pltpu.VMEM((TENSOR, OWN, D), BF16),
@@ -389,15 +397,14 @@
             pltpu.VMEM((TENSOR, OWN, D), BF16),
             pltpu.VMEM((TENSOR, OWN, D), BF16),
             pltpu.VMEM((OWN, D), BF16),
-            pltpu.VMEM((TENSOR, OWN, D), BF16),
-            pltpu.VMEM((TENSOR, OWN, D), BF16),
-            pltpu.VMEM((GUIDE, ROWS, D), BF16),
+            pltpu.VMEM((GUIDE, TENSOR, OWN, D), BF16),
             pltpu.VMEM((ROWS, D), BF16),
+            pltpu.VMEM((ROWS, VOCAB_LOCAL), F32),
             pltpu.VMEM((8, ROWS), F32),
             pltpu.VMEM((GUIDE * TENSOR, 8, ROWS), F32),
             dma((14,)),
-            dma((10,)),
-            dma((10,)),
+            dma((12,)),
+            dma((12,)),
         ],
         compiler_params=pltpu.CompilerParams(
             collective_id=0, has_side_effects=True, vmem_limit_bytes=60 * 1024 * 1024

time: 76.5 us -> 69.1 us (0.903)
  Pallas kernels: 75.7 us -> 68.3 us
    pallas_call x1, Pallas kernels: 73.4 us -> 66 us  [local(): pl.pallas_call(kernel, name='decode_step', out_shape=(jax.ShapeDtypeStruc...]
where the time goes in v3:
time: 69.1 us; the launch traced here: 68.9 us
  Pallas kernels  68.3 us (99%)
    pallas_call x1, Pallas kernels, local(): pl.pallas_call(kernel, name='decode_step', out_shape=(jax.ShapeDtypeStruc...  66 us
    pallas_call x1, Pallas kernels, local(): pl.pallas_call(settle, name='settle', out_shape=(jax.ShapeDtypeStruct((RO...  2.32 us

profile of v3, /device:TPU:1, one launch (start us, length us, event | category | flops | bytes accessed | tf_op | source)
XLA Modules:
  0.0 68.9 jit_solution(264668795928195172)
XLA Ops:
  0.6 66.0 %decode_step.1 = (f32[128,2048]{1,0:T(8,128)}, f32[128,128]{1,0:T(8,128)}, bf16[8,2048]{1,0:T(8,128)(2,1)}, bf16[192,128]{1,0:T(8,128)(2,1)}) custom-call(bf16[1,8,2048]{2,1,0:T(8,128)(2,1)} %stream.1, f32[1,2048]{1,0:T(1,128)} %bitcast.12, bf16[192,2048]{1,0:T(8,128)(2,1)} %bitcast.10, bf16[1,8,1024,512]{3,2,1,0:T(8,128)(2,1)} %keys.1, ...), custom_call_target="tpu_custom_call" | custom-call | tf_op jit(solution)/shard_map/decode_step/pallas_call | solution.py:361
  66.6 2.3 %settle.1 = (f32[128,2048]{1,0:T(8,128)}, bf16[8,2048]{1,0:T(8,128)(2,1)}, bf16[192,128]{1,0:T(8,128)(2,1)}) custom-call(f32[128,2048]{1,0:T(8,128)} %get-tuple-element.10.guided, f32[128,128]{1,0:T(8,128)} %get-tuple-element.11.level, bf16[8,2048]{1,0:T(8,128)(2,1)} %get-tuple-element.12.layer_rows, bf16[192,128]{1,0:T(8,128)(2,1)} %get-tuple-element.13.next_rows), custom_call_target="tpu_custom_call" | custom-call | tf_op jit(solution)/shard_map/settle/pallas_call | solution.py:417

commit v4 on v3

--- a/solution.py
+++ b/solution.py
@@ -81,13 +81,9 @@
     ).start()
 
 
-def distance(step):
-    return min(step, SIDE - step)
-
-
-OFFSETS = sorted(
-    ((dy, dx) for dy in range(SIDE) for dx in range(SIDE)),
-    key=lambda at: -distance(at[0]) - distance(at[1]),
+OFFSETS = (
+    (2, 2), (1, 2), (2, 1), (3, 2), (2, 3), (1, 1), (3, 3), (1, 3), (3, 1),
+    (0, 2), (2, 0), (0, 1), (1, 0), (0, 3), (3, 0), (0, 0),
 )
 
 
@@ -96,8 +92,8 @@
     final_gain, lm_head, next_gain, w_next, counts, levels,
     guided_all, level_out, layer_out, next_qkv,
     stream_v, gains_v, w_qkv_v, keys_v, values_v, w_out_v, w_gate_v, w_up_v, w_down_v, lm_head_v, w_next_v,
-    stream_all, proj, request_side, queries, scores, probs, mixed, head_out, head_all, w_cols, after_own, after_all, after_rows,
-    partial, shares, layer_own, layer_all, final_rows, cond_all, stats_own, stats_all,
+    lm_head_t, stream_all, proj, request_side, queries, scores, probs, mixed, head_out, head_all, w_cols, after_own, after_all, after_rows,
+    partial, shares, layer_own, layer_all, final_rows, cond_all, next_own, stats_own, stats_all,
     load_sems, sends, recvs,
 ):
     guide = lax.axis_index("guide")
@@ -232,6 +228,14 @@
             [mixed[g, :, here] for g in range(GROUPS)], axis=1
         ).astype(BF16)
     cross(3, lambda there: head_out, head_all.at[me], head_all)
+    ready(13)
+
+    def turn_head(step, carry):
+        here = pl.ds(pl.multiple_of(step * VOCAB_STEP, VOCAB_STEP), VOCAB_STEP)
+        lm_head_t[:, here] = lm_head_v[here, :].T
+        return carry
+
+    lax.fori_loop(0, VOCAB_LOCAL // VOCAB_STEP, turn_head, 0)
     drain(w_cols.at[:, half], recvs.at[11])
     drain(head_all, recvs.at[3])
 
@@ -273,7 +277,7 @@
         level = jnp.where(request >= bound, levels[t].astype(F32), level)
         bound = bound + counts[t]
     weight = level * 0.25
-    ready(10, 11, 12, 13)
+    ready(10, 11, 12)
 
     def arrive(branch):
         @pl.when(guide == branch)
@@ -287,8 +291,8 @@
             final_rows[at * OWN : (at + SIDE) * OWN] = rms_norm(wide, gains_v[3]).astype(BF16)
 
     def logits(step):
-        return lax.dot_general(
-            final_rows[...], lm_head_v[step * VOCAB_STEP : (step + 1) * VOCAB_STEP], NT,
+        return jnp.dot(
+            final_rows[...], lm_head_t[:, step * VOCAB_STEP : (step + 1) * VOCAB_STEP],
             preferred_element_type=F32,
         )
 
@@ -325,13 +329,18 @@
         send(stats_own, stats_all.at[place], sends.at[7], recvs.at[7], {"tensor": there})
     finish.append(lambda: drain(stats_all.at[pl.ds(0, GUIDE * TENSOR - 1)], sends.at[7]))
 
-    layer_out[...] = layer_all[guide, me]
+    copy = pltpu.make_async_copy(layer_all.at[guide, me], layer_out, load_sems.at[steps])
+    copy.start()
+    finish.append(copy.wait)
     for at in range(0, TENSOR, SIDE):
         wide = layer_all[guide, pl.ds(at, SIDE)].astype(F32).reshape(SIDE * OWN, D)
         final_rows[at * OWN : (at + SIDE) * OWN] = rms_norm(wide, gains_v[2]).astype(BF16)
-    next_qkv[...] = lax.dot_general(
+    next_own[...] = lax.dot_general(
         w_next_v[...], final_rows[...], NT, preferred_element_type=F32
     ).astype(BF16)
+    copy = pltpu.make_async_copy(next_own, next_qkv, load_sems.at[steps + 1])
+    copy.start()
+    finish.append(copy.wait)
     drain(stats_all.at[pl.ds(0, GUIDE * TENSOR - 1)], recvs.at[7])
     peaks = stats_all[:, 0, :]
     peak = jnp.max(peaks, axis=0, keepdims=True)
@@ -368,7 +377,7 @@
             jax.ShapeDtypeStruct((QKV_LOCAL, ROWS), BF16),
         ),
         in_specs=[hbm] * 5 + [smem] + [hbm] * 9 + [smem] * 2,
-        out_specs=(hbm, vmem, vmem, vmem),
+        out_specs=(hbm, vmem, hbm, hbm),
         scratch_shapes=[
             pltpu.VMEM((OWN, D), BF16),
             pltpu.VMEM((4, 1, D), F32),
@@ -381,6 +390,7 @@
             pltpu.VMEM((FF_LOCAL, D), BF16),
             pltpu.VMEM((VOCAB_LOCAL, D), BF16),
             pltpu.VMEM((QKV_LOCAL, D), BF16),
+            pltpu.VMEM((D, VOCAB_LOCAL), BF16),
             pltpu.VMEM((TENSOR, OWN, D), BF16),
             pltpu.VMEM((TENSOR, OWN, QKV_LOCAL), BF16),
             pltpu.VMEM((TENSOR, OWN, QKV_LOCAL), BF16),
@@ -400,6 +410,7 @@
             pltpu.VMEM((GUIDE, TENSOR, OWN, D), BF16),
             pltpu.VMEM((ROWS, D), BF16),
             pltpu.VMEM((ROWS, VOCAB_LOCAL), F32),
+            pltpu.VMEM((QKV_LOCAL, ROWS), BF16),
             pltpu.VMEM((8, ROWS), F32),
             pltpu.VMEM((GUIDE * TENSOR, 8, ROWS), F32),
             dma((14,)),

time: 69.1 us -> 66.2 us (0.958)
  Pallas kernels: 68.3 us -> 65.4 us
    pallas_call x1, Pallas kernels: 66 us -> 63.1 us  [local(): pl.pallas_call(kernel, name='decode_step', out_shape=(jax.ShapeDtypeStruc...]
where the time goes in v4:
time: 66.2 us; the launch traced here: 66 us
  Pallas kernels  65.4 us (99%)
    pallas_call x1, Pallas kernels, local(): pl.pallas_call(kernel, name='decode_step', out_shape=(jax.ShapeDtypeStruc...  63.1 us
    pallas_call x1, Pallas kernels, local(): pl.pallas_call(settle, name='settle', out_shape=(jax.ShapeDtypeStruct((RO...  2.32 us

profile of v4, /device:TPU:1, one launch (start us, length us, event | category | flops | bytes accessed | tf_op | source)
XLA Modules:
  0.0 66.0 jit_solution(15105788529485662047)
XLA Ops:
  0.6 63.1 %decode_step.1 = (f32[128,2048]{1,0:T(8,128)}, f32[128,128]{1,0:T(8,128)}, bf16[8,2048]{1,0:T(8,128)(2,1)}, bf16[192,128]{1,0:T(8,128)(2,1)}) custom-call(bf16[1,8,2048]{2,1,0:T(8,128)(2,1)} %stream.1, f32[1,2048]{1,0:T(1,128)} %bitcast.12, bf16[192,2048]{1,0:T(8,128)(2,1)} %bitcast.10, bf16[1,8,1024,512]{3,2,1,0:T(8,128)(2,1)} %keys.1, ...), custom_call_target="tpu_custom_call" | custom-call | tf_op jit(solution)/shard_map/decode_step/pallas_call | solution.py:370
  63.7 2.3 %settle.1 = (f32[128,2048]{1,0:T(8,128)}, bf16[8,2048]{1,0:T(8,128)(2,1)}, bf16[192,128]{1,0:T(8,128)(2,1)}) custom-call(f32[128,2048]{1,0:T(8,128)} %get-tuple-element.10.guided, f32[128,128]{1,0:T(8,128)} %get-tuple-element.11.level, bf16[8,2048]{1,0:T(8,128)(2,1)} %get-tuple-element.12.layer_rows, bf16[192,128]{1,0:T(8,128)(2,1)} %get-tuple-element.13.next_rows), custom_call_target="tpu_custom_call" | custom-call | tf_op jit(solution)/shard_map/settle/pallas_call | solution.py:428

commit v5 on v4

--- a/solution.py
+++ b/solution.py
@@ -24,7 +24,7 @@
 SIDE = 4
 TENSOR = 16
 GUIDE = 2
-VOCAB_STEP = 256
+VOCAB_STEP = 512
 
 EPSILON = 1e-05
 ROPE_BASE = 500000.0
@@ -85,6 +85,8 @@
     (2, 2), (1, 2), (2, 1), (3, 2), (2, 3), (1, 1), (3, 3), (1, 3), (3, 1),
     (0, 2), (2, 0), (0, 1), (1, 0), (0, 3), (3, 0), (0, 0),
 )
+
+FAR = 5
 
 
 def kernel(
@@ -137,16 +139,16 @@
         for k in which:
             left.pop(k).wait()
 
-    def cross(phase, part, dst, whole, early=None):
+    def cross(phase, part, dst, whole, early=(), apart=10):
         for offset, there in zip(OFFSETS, chips):
-            landed = recvs.at[10] if offset == early else recvs.at[phase]
+            landed = recvs.at[apart] if offset in early else recvs.at[phase]
             send(part(there), dst, sends.at[phase], landed, {"guide": other, "tensor": there})
         finish.append(lambda: drain(whole, sends.at[phase]))
 
     pl.semaphore_wait(barrier, 2 * TENSOR - 1)
     ready(0)
     pl.when(guide == 1)(lambda: drain(stream_all.at[0], recvs.at[10]))
-    cross(0, lambda there: stream_v, stream_all.at[me], stream_all, early=(0, 1))
+    cross(0, lambda there: stream_v, stream_all.at[me], stream_all, early=((0, 1),))
     pl.when(guide == 0)(lambda: drain(stream_all.at[0], recvs.at[10]))
 
     row = lax.broadcasted_iota(jnp.int32, (OWN, 2 * HEAD_DIM), 0)
@@ -268,7 +270,10 @@
     for k in range(1, TENSOR):
         share = share + shares[k].astype(F32)
     layer_own[...] = (wide + share).astype(BF16)
-    cross(6, lambda there: layer_own, layer_all.at[other, me], layer_all.at[other])
+    cross(
+        6, lambda there: layer_own, layer_all.at[other, me], layer_all.at[other],
+        early=OFFSETS[FAR:], apart=12,
+    )
 
     request = batch * ROWS + lax.broadcasted_iota(jnp.int32, (ROWS, VOCAB_STEP), 0)
     level = jnp.full((ROWS, VOCAB_STEP), levels[0].astype(F32))
@@ -282,8 +287,14 @@
     def arrive(branch):
         @pl.when(guide == branch)
         def _():
-            drain(layer_all.at[branch], recvs.at[6])
-            send(layer_all.at[branch], layer_all.at[branch], sends.at[9], recvs.at[9], {"guide": other})
+            drain(layer_all.at[branch, pl.ds(FAR, TENSOR - FAR)], recvs.at[12])
+            for there in chips[FAR:]:
+                block = layer_all.at[branch, there]
+                send(block, block, sends.at[9], recvs.at[9], {"guide": other})
+            drain(layer_all.at[branch, pl.ds(0, FAR)], recvs.at[6])
+            for there in chips[:FAR]:
+                block = layer_all.at[branch, there]
+                send(block, block, sends.at[9], recvs.at[9], {"guide": other})
 
         pl.when(guide != branch)(lambda: drain(layer_all.at[branch], recvs.at[9]))
         for at in range(0, TENSOR, SIDE):
@@ -415,7 +426,7 @@
             pltpu.VMEM((GUIDE * TENSOR, 8, ROWS), F32),
             dma((14,)),
             dma((12,)),
-            dma((12,)),
+            dma((13,)),
         ],
         compiler_params=pltpu.CompilerParams(
             collective_id=0, has_side_effects=True, vmem_limit_bytes=60 * 1024 * 1024

time: 66.2 us -> 65.9 us (level)
  no operation moved by 1% of the time
where the time goes in v5:
time: 65.9 us; the launch traced here: 65.7 us
  Pallas kernels  65.1 us (99%)
    pallas_call x1, Pallas kernels, local(): pl.pallas_call(kernel, name='decode_step', out_shape=(jax.ShapeDtypeStruc...  62.7 us
    pallas_call x1, Pallas kernels, local(): pl.pallas_call(settle, name='settle', out_shape=(jax.ShapeDtypeStruct((RO...  2.32 us

profile of v5, /device:TPU:1, one launch (start us, length us, event | category | flops | bytes accessed | tf_op | source)
XLA Modules:
  0.0 65.7 jit_solution(15703554377240480152)
XLA Ops:
  0.6 62.7 %decode_step.1 = (f32[128,2048]{1,0:T(8,128)}, f32[128,128]{1,0:T(8,128)}, bf16[8,2048]{1,0:T(8,128)(2,1)}, bf16[192,128]{1,0:T(8,128)(2,1)}) custom-call(bf16[1,8,2048]{2,1,0:T(8,128)(2,1)} %stream.1, f32[1,2048]{1,0:T(1,128)} %bitcast.12, bf16[192,2048]{1,0:T(8,128)(2,1)} %bitcast.10, bf16[1,8,1024,512]{3,2,1,0:T(8,128)(2,1)} %keys.1, ...), custom_call_target="tpu_custom_call" | custom-call | tf_op jit(solution)/shard_map/decode_step/pallas_call | solution.py:381
  63.4 2.3 %settle.1 = (f32[128,2048]{1,0:T(8,128)}, bf16[8,2048]{1,0:T(8,128)(2,1)}, bf16[192,128]{1,0:T(8,128)(2,1)}) custom-call(f32[128,2048]{1,0:T(8,128)} %get-tuple-element.10.guided, f32[128,128]{1,0:T(8,128)} %get-tuple-element.11.level, bf16[8,2048]{1,0:T(8,128)(2,1)} %get-tuple-element.12.layer_rows, bf16[192,128]{1,0:T(8,128)(2,1)} %get-tuple-element.13.next_rows), custom_call_target="tpu_custom_call" | custom-call | tf_op jit(solution)/shard_map/settle/pallas_call | solution.py:439
